TPU v7x, 256 devices: a whole 4x4x8 slice. The times are simulated.
256 devices in a mesh: tm: 32 (over z, x), elem: 8 (over y, core).
Axes of the slice: x: 4, y: 4, z: 8, core: 2. Of those that a mesh axis runs over, the one named last changes fastest.
Arguments:
- modal_coords: bfloat16 [16384, 512], P('tm'), may hold values from -6 to 6
- stress_modes: bfloat16 [3, 512, 16384], P(None, None, 'elem'), may hold values from -0.375 to 0.375
- step_decay: float32 [16384, 512], P('tm'), may hold values from 0 to 1, as said below
- ply_layup: int32 [128], P('elem'), may hold values from 0 to 15
- lin_table: float32 [16, 2], replicated, may hold values from -0.03 to 0.03
- quad_table: float32 [16, 3], replicated, may hold values from 0.0005 to 0.004
- base_index: float32 [16], replicated, may hold values from 0.9 to 1.1
Outputs:
- column_ks: float32 [16384], P('elem')
- adjoint_states: float32 [16384, 512], P('tm')
Inputs may be any that keep to these rules, and one draw needn't show every extreme that they name: `step_decay`: per-step factors of the modal adjoint states.
All inputs are finite; a program needn't handle non-finite values.
Results may differ from a plain program's by a relative error of at most 0.0027.
Values sent between devices are 32-bit elements; how exact they have to be, the bound alone decides.
A program may use at most 128 MiB of HBM per device.

v0:
```python
import jax
import jax.numpy as jnp
from jax import lax
from jax.sharding import PartitionSpec as P

COL_BLOCK = 128
LAYUPS = 16


sharpness = 100.0


def from_behind(block, axis, distance):
    devices = range(lax.axis_size(axis))
    route = [(i - distance, i) for i in devices if i - distance in devices]
    return lax.ppermute(block, axis, route)


def column_coefs(ply_layup, lin_table, quad_table, base_index):
    levels = jnp.arange(LAYUPS, dtype=jnp.int32)
    onehot = (ply_layup[:, None] == levels[None, :]).astype(jnp.float32)
    coef_table = jnp.concatenate([lin_table, quad_table, base_index[:, None]], axis=1)
    per_block = jnp.dot(onehot, coef_table, precision=lax.Precision.HIGHEST)
    return jnp.repeat(per_block, COL_BLOCK, axis=0).T


def failure_terms(stress, col_coefs):
    stress_one = stress[0]
    stress_two = stress[1]
    stress_shear = stress[2]
    lin_one = col_coefs[0][None, :]
    lin_two = col_coefs[1][None, :]
    quad_one = col_coefs[2][None, :]
    quad_two = col_coefs[3][None, :]
    quad_shear = col_coefs[4][None, :]
    static = col_coefs[5][None, :]
    cross_term = -0.5 * jnp.sqrt(quad_one * quad_two)
    failure_index = (
        static
        + lin_one * stress_one
        + lin_two * stress_two
        + quad_one * stress_one * stress_one
        + quad_two * stress_two * stress_two
        + quad_shear * stress_shear * stress_shear
        + 2.0 * cross_term * stress_one * stress_two
    )
    slopes = (
        lin_one + 2.0 * quad_one * stress_one + 2.0 * cross_term * stress_two,
        lin_two + 2.0 * quad_two * stress_two + 2.0 * cross_term * stress_one,
        2.0 * quad_shear * stress_shear,
    )
    return (failure_index, slopes)


def compose(farther, nearer):
    return (nearer[0] * farther[0], nearer[1] + nearer[0] * farther[1])


def chain_back(decay_rows, load_rows, time_axis):
    carry_scale, offset = lax.associative_scan(
        compose, (decay_rows, load_rows), reverse=True, axis=time_axis
    )
    head_carry = lax.index_in_dim(carry_scale, 0, time_axis, keepdims=False)
    head_offset = lax.index_in_dim(offset, 0, time_axis, keepdims=False)
    incoming = jnp.zeros_like(head_offset)
    for handoff_turn in range(lax.axis_size("tm") - 1):
        incoming = from_behind(head_offset + head_carry * incoming, "tm", -1)
    return offset + carry_scale * jnp.expand_dims(incoming, time_axis)


def body(modal_coords, stress_modes, step_decay, ply_layup, lin_table, quad_table, base_index):
    col_coefs = column_coefs(ply_layup, lin_table, quad_table, base_index)
    stress = jnp.einsum(
        "tm,kmc->ktc", modal_coords, stress_modes, preferred_element_type=jnp.float32
    )
    failure_index, slopes = failure_terms(stress, col_coefs)
    peak_value = lax.pmax(jnp.max(failure_index, axis=0), "tm")
    scaled_exp = jnp.exp(sharpness * (failure_index - peak_value[None, :]))
    mass_total = lax.psum(jnp.sum(scaled_exp, axis=0), "tm")
    column_ks = peak_value + jnp.log(mass_total) / sharpness
    weight = sharpness * scaled_exp / mass_total[None, :]
    sensitivity = jnp.stack([weight * slopes[0], weight * slopes[1], weight * slopes[2]]).astype(
        jnp.bfloat16
    )
    local_loads = lax.dot_general(
        sensitivity, stress_modes, (((0, 2), (0, 2)), ((), ())), preferred_element_type=jnp.float32
    )
    load_rows = lax.psum(local_loads, "elem")
    adjoint = chain_back(step_decay, load_rows, 0)
    return (column_ks, adjoint)


def solution(mesh):
    return jax.shard_map(
        body,
        mesh=mesh,
        in_specs=(P("tm", None), P(None, None, "elem"), P("tm", None), P("elem"), P(), P(), P()),
        out_specs=(P("elem"), P("tm", None)),
        check_vma=False,
    )
```

profile of v0, /device:TPU:128, one launch (start us, length us, event | category | flops | bytes accessed | tf_op | source)
XLA Modules:
  0.0 581.7 jit_solution(983731500119498555)
XLA Ops:
  8.4 5.5 convolution_bitcast_fusion
  13.9 4.3 fusion.46
  19.7 73.0 %pmax.7 = f32[2048]{0:T(1024)S(1)} all-reduce(f32[2048]{0:T(1024)S(1)} %get-tuple-element.4), channel_id=1, replica_groups=mesh['tm'=32,'elem'=8] {'tm'}, use_global_device_ids=true, to_apply=%region_1.0 | all-reduce | flops 2048 | bytes 16384 | tf_op jit(solution)/shard_map/pmax | solution.py:77
  92.7 2.9 exponential_reduce_fusion
  95.6 70.8 %psum.14 = f32[2048]{0:T(1024)S(1)} all-reduce(f32[2048]{0:T(1024)S(1)} %exponential_reduce_fusion), channel_id=1, replica_groups=mesh['tm'=32,'elem'=8] {'tm'}, use_global_device_ids=true, to_apply=%region_3.0 | all-reduce | flops 2048 | bytes 16384 | tf_op jit(solution)/shard_map/psum | solution.py:79
  166.5 7.8 %multiply_convert_fusion.2 = (bf16[1,512,2048]{2,1,0:T(8,128)(2,1)}, f32[1,512,2048]{2,1,0:T(8,128)S(1)}) fusion(f32[3,512,2048]{2,1,0:T(8,128)} %copy-done.2, f32[2048]{0:T(1024)S(1)} %bitcast.140, f32[2048]{0:T(1024)S(1)} %bitcast.123, f32[2048]{0:T(1024)S(1)} %bitcast.135, f32[2048]{0:T(1024)S(1)} %psum.14, f32[2048]{0:T(1024)S(1)} %pmax.7, ...), kind=kLoop, calls=%fused_computation.34 | loop fusion | flops 27262976 | bytes 18956288 | tf_op jit(solution)/shard_map/convert
  175.4 3.7 multiply_convert_fusion.1
  179.2 7.5 %fusion.21 = f32[512,512]{1,0:T(8,128)} fusion(bf16[3,512,2048]{2,1,0:T(8,128)(2,1)S(1)} %bitcast.58, bf16[1,512,2048]{2,1,0:T(8,128)(2,1)} %get-tuple-element.7, bf16[1,512,2048]{2,1,0:T(8,128)(2,1)} %get-tuple-element.6, bf16[1,512,2048]{2,1,0:T(8,128)(2,1)} %get-tuple-element.2), kind=kOutput, calls=%fused_computation.36 | convolution fusion | flops 3227516928 | bytes 13631488 | tf_op jit(solution)/shard_map/dot_general | solution.py:85
  188.9 2.9 slice.328
  191.9 63.0 %all-reduce.38.cloned.1.call-done = f32[512,512]{1,0:T(8,128)} async-done(((f32[512,512]{1,0:T(8,128)}), f32[512,512]{1,0:T(8,128)}) %all-reduce.38.cloned.1.call-update) | async-done | bytes 1048592 | tf_op jit(solution)/shard_map/psum | solution.py:88
  254.9 3.0 slice.329
  258.2 3.0 slice.333
  267.6 3.7 slice.325
  271.3 4.9 slice.326
  279.6 4.6 pad.127
  288.4 4.5 collective-permute-start
  294.3 7.5 %collective-permute-start.1 = (f32[512]{0:T(512)S(1)}, f32[512]{0:T(512)S(1)}, u32[]{:S(2)}, u32[]{:S(2)}) collective-permute-start(f32[512]{0:T(512)S(1)} %multiply_add_fusion.39), channel_id=1, source_target_pairs={{8,0},{16,8},{24,16},{32,24},{40,32},{48,40},{56,48},{64,56},{72,6... | collective-permute-start | bytes 6152 | tf_op jit(solution)/shard_map/ppermute | solution.py:16
  303.0 7.5 %collective-permute-start.2 = (f32[512]{0:T(512)S(1)}, f32[512]{0:T(512)S(1)}, u32[]{:S(2)}, u32[]{:S(2)}) collective-permute-start(f32[512]{0:T(512)S(1)} %multiply_add_fusion.38), channel_id=1, source_target_pairs={{8,0},{16,8},{24,16},{32,24},{40,32},{48,40},{56,48},{64,56},{72,6... | collective-permute-start | bytes 6152 | tf_op jit(solution)/shard_map/ppermute | solution.py:16
  311.8 7.5 %collective-permute-start.3 = (f32[512]{0:T(512)S(1)}, f32[512]{0:T(512)S(1)}, u32[]{:S(2)}, u32[]{:S(2)}) collective-permute-start(f32[512]{0:T(512)S(1)} %multiply_add_fusion.37), channel_id=1, source_target_pairs={{8,0},{16,8},{24,16},{32,24},{40,32},{48,40},{56,48},{64,56},{72,6... | collective-permute-start | bytes 6152 | tf_op jit(solution)/shard_map/ppermute | solution.py:16
  320.6 7.5 %collective-permute-start.4 = (f32[512]{0:T(512)S(1)}, f32[512]{0:T(512)S(1)}, u32[]{:S(2)}, u32[]{:S(2)}) collective-permute-start(f32[512]{0:T(512)S(1)} %multiply_add_fusion.36), channel_id=1, source_target_pairs={{8,0},{16,8},{24,16},{32,24},{40,32},{48,40},{56,48},{64,56},{72,6... | collective-permute-start | bytes 6152 | tf_op jit(solution)/shard_map/ppermute | solution.py:16
  329.4 7.5 %collective-permute-start.5 = (f32[512]{0:T(512)S(1)}, f32[512]{0:T(512)S(1)}, u32[]{:S(2)}, u32[]{:S(2)}) collective-permute-start(f32[512]{0:T(512)S(1)} %multiply_add_fusion.35), channel_id=1, source_target_pairs={{8,0},{16,8},{24,16},{32,24},{40,32},{48,40},{56,48},{64,56},{72,6... | collective-permute-start | bytes 6152 | tf_op jit(solution)/shard_map/ppermute | solution.py:16
  338.2 7.5 %collective-permute-start.6 = (f32[512]{0:T(512)S(1)}, f32[512]{0:T(512)S(1)}, u32[]{:S(2)}, u32[]{:S(2)}) collective-permute-start(f32[512]{0:T(512)S(1)} %multiply_add_fusion.34), channel_id=1, source_target_pairs={{8,0},{16,8},{24,16},{32,24},{40,32},{48,40},{56,48},{64,56},{72,6... | collective-permute-start | bytes 6152 | tf_op jit(solution)/shard_map/ppermute | solution.py:16
  347.0 7.5 %collective-permute-start.7 = (f32[512]{0:T(512)S(1)}, f32[512]{0:T(512)S(1)}, u32[]{:S(2)}, u32[]{:S(2)}) collective-permute-start(f32[512]{0:T(512)S(1)} %multiply_add_fusion.33), channel_id=1, source_target_pairs={{8,0},{16,8},{24,16},{32,24},{40,32},{48,40},{56,48},{64,56},{72,6... | collective-permute-start | bytes 6152 | tf_op jit(solution)/shard_map/ppermute | solution.py:16
  355.8 7.5 %collective-permute-start.8 = (f32[512]{0:T(512)S(1)}, f32[512]{0:T(512)S(1)}, u32[]{:S(2)}, u32[]{:S(2)}) collective-permute-start(f32[512]{0:T(512)S(1)} %multiply_add_fusion.32), channel_id=1, source_target_pairs={{8,0},{16,8},{24,16},{32,24},{40,32},{48,40},{56,48},{64,56},{72,6... | collective-permute-start | bytes 6152 | tf_op jit(solution)/shard_map/ppermute | solution.py:16
  364.6 7.5 %collective-permute-start.9 = (f32[512]{0:T(512)S(1)}, f32[512]{0:T(512)S(1)}, u32[]{:S(2)}, u32[]{:S(2)}) collective-permute-start(f32[512]{0:T(512)S(1)} %multiply_add_fusion.31), channel_id=1, source_target_pairs={{8,0},{16,8},{24,16},{32,24},{40,32},{48,40},{56,48},{64,56},{72,6... | collective-permute-start | bytes 6152 | tf_op jit(solution)/shard_map/ppermute | solution.py:16
  373.4 7.5 %collective-permute-start.10 = (f32[512]{0:T(512)S(1)}, f32[512]{0:T(512)S(1)}, u32[]{:S(2)}, u32[]{:S(2)}) collective-permute-start(f32[512]{0:T(512)S(1)} %multiply_add_fusion.30), channel_id=1, source_target_pairs={{8,0},{16,8},{24,16},{32,24},{40,32},{48,40},{56,48},{64,56},{72,6... | collective-permute-start | bytes 6152 | tf_op jit(solution)/shard_map/ppermute | solution.py:16
  382.2 7.5 %collective-permute-start.11 = (f32[512]{0:T(512)S(1)}, f32[512]{0:T(512)S(1)}, u32[]{:S(2)}, u32[]{:S(2)}) collective-permute-start(f32[512]{0:T(512)S(1)} %multiply_add_fusion.29), channel_id=1, source_target_pairs={{8,0},{16,8},{24,16},{32,24},{40,32},{48,40},{56,48},{64,56},{72,6... | collective-permute-start | bytes 6152 | tf_op jit(solution)/shard_map/ppermute | solution.py:16
  391.0 7.5 %collective-permute-start.12 = (f32[512]{0:T(512)S(1)}, f32[512]{0:T(512)S(1)}, u32[]{:S(2)}, u32[]{:S(2)}) collective-permute-start(f32[512]{0:T(512)S(1)} %multiply_add_fusion.28), channel_id=1, source_target_pairs={{8,0},{16,8},{24,16},{32,24},{40,32},{48,40},{56,48},{64,56},{72,6... | collective-permute-start | bytes 6152 | tf_op jit(solution)/shard_map/ppermute | solution.py:16
  399.8 7.5 %collective-permute-start.13 = (f32[512]{0:T(512)S(1)}, f32[512]{0:T(512)S(1)}, u32[]{:S(2)}, u32[]{:S(2)}) collective-permute-start(f32[512]{0:T(512)S(1)} %multiply_add_fusion.27), channel_id=1, source_target_pairs={{8,0},{16,8},{24,16},{32,24},{40,32},{48,40},{56,48},{64,56},{72,6... | collective-permute-start | bytes 6152 | tf_op jit(solution)/shard_map/ppermute | solution.py:16
  408.6 7.5 %collective-permute-start.14 = (f32[512]{0:T(512)S(1)}, f32[512]{0:T(512)S(1)}, u32[]{:S(2)}, u32[]{:S(2)}) collective-permute-start(f32[512]{0:T(512)S(1)} %multiply_add_fusion.26), channel_id=1, source_target_pairs={{8,0},{16,8},{24,16},{32,24},{40,32},{48,40},{56,48},{64,56},{72,6... | collective-permute-start | bytes 6152 | tf_op jit(solution)/shard_map/ppermute | solution.py:16
  417.3 7.5 %collective-permute-start.15 = (f32[512]{0:T(512)S(1)}, f32[512]{0:T(512)S(1)}, u32[]{:S(2)}, u32[]{:S(2)}) collective-permute-start(f32[512]{0:T(512)S(1)} %multiply_add_fusion.25), channel_id=1, source_target_pairs={{8,0},{16,8},{24,16},{32,24},{40,32},{48,40},{56,48},{64,56},{72,6... | collective-permute-start | bytes 6152 | tf_op jit(solution)/shard_map/ppermute | solution.py:16
  426.1 7.5 %collective-permute-start.16 = (f32[512]{0:T(512)S(1)}, f32[512]{0:T(512)S(1)}, u32[]{:S(2)}, u32[]{:S(2)}) collective-permute-start(f32[512]{0:T(512)S(1)} %multiply_add_fusion.24), channel_id=1, source_target_pairs={{8,0},{16,8},{24,16},{32,24},{40,32},{48,40},{56,48},{64,56},{72,6... | collective-permute-start | bytes 6152 | tf_op jit(solution)/shard_map/ppermute | solution.py:16
  434.9 7.5 %collective-permute-start.17 = (f32[512]{0:T(512)S(1)}, f32[512]{0:T(512)S(1)}, u32[]{:S(2)}, u32[]{:S(2)}) collective-permute-start(f32[512]{0:T(512)S(1)} %multiply_add_fusion.23), channel_id=1, source_target_pairs={{8,0},{16,8},{24,16},{32,24},{40,32},{48,40},{56,48},{64,56},{72,6... | collective-permute-start | bytes 6152 | tf_op jit(solution)/shard_map/ppermute | solution.py:16
  443.7 7.5 %collective-permute-start.18 = (f32[512]{0:T(512)S(1)}, f32[512]{0:T(512)S(1)}, u32[]{:S(2)}, u32[]{:S(2)}) collective-permute-start(f32[512]{0:T(512)S(1)} %multiply_add_fusion.22), channel_id=1, source_target_pairs={{8,0},{16,8},{24,16},{32,24},{40,32},{48,40},{56,48},{64,56},{72,6... | collective-permute-start | bytes 6152 | tf_op jit(solution)/shard_map/ppermute | solution.py:16
  452.5 7.5 %collective-permute-start.19 = (f32[512]{0:T(512)S(1)}, f32[512]{0:T(512)S(1)}, u32[]{:S(2)}, u32[]{:S(2)}) collective-permute-start(f32[512]{0:T(512)S(1)} %multiply_add_fusion.21), channel_id=1, source_target_pairs={{8,0},{16,8},{24,16},{32,24},{40,32},{48,40},{56,48},{64,56},{72,6... | collective-permute-start | bytes 6152 | tf_op jit(solution)/shard_map/ppermute | solution.py:16
  461.3 7.5 %collective-permute-start.20 = (f32[512]{0:T(512)S(1)}, f32[512]{0:T(512)S(1)}, u32[]{:S(2)}, u32[]{:S(2)}) collective-permute-start(f32[512]{0:T(512)S(1)} %multiply_add_fusion.20), channel_id=1, source_target_pairs={{8,0},{16,8},{24,16},{32,24},{40,32},{48,40},{56,48},{64,56},{72,6... | collective-permute-start | bytes 6152 | tf_op jit(solution)/shard_map/ppermute | solution.py:16
  470.1 7.5 %collective-permute-start.21 = (f32[512]{0:T(512)S(1)}, f32[512]{0:T(512)S(1)}, u32[]{:S(2)}, u32[]{:S(2)}) collective-permute-start(f32[512]{0:T(512)S(1)} %multiply_add_fusion.19), channel_id=1, source_target_pairs={{8,0},{16,8},{24,16},{32,24},{40,32},{48,40},{56,48},{64,56},{72,6... | collective-permute-start | bytes 6152 | tf_op jit(solution)/shard_map/ppermute | solution.py:16
  478.9 7.5 %collective-permute-start.22 = (f32[512]{0:T(512)S(1)}, f32[512]{0:T(512)S(1)}, u32[]{:S(2)}, u32[]{:S(2)}) collective-permute-start(f32[512]{0:T(512)S(1)} %multiply_add_fusion.18), channel_id=1, source_target_pairs={{8,0},{16,8},{24,16},{32,24},{40,32},{48,40},{56,48},{64,56},{72,6... | collective-permute-start | bytes 6152 | tf_op jit(solution)/shard_map/ppermute | solution.py:16
  487.7 7.5 %collective-permute-start.23 = (f32[512]{0:T(512)S(1)}, f32[512]{0:T(512)S(1)}, u32[]{:S(2)}, u32[]{:S(2)}) collective-permute-start(f32[512]{0:T(512)S(1)} %multiply_add_fusion.17), channel_id=1, source_target_pairs={{8,0},{16,8},{24,16},{32,24},{40,32},{48,40},{56,48},{64,56},{72,6... | collective-permute-start | bytes 6152 | tf_op jit(solution)/shard_map/ppermute | solution.py:16
  496.5 7.5 %collective-permute-start.24 = (f32[512]{0:T(512)S(1)}, f32[512]{0:T(512)S(1)}, u32[]{:S(2)}, u32[]{:S(2)}) collective-permute-start(f32[512]{0:T(512)S(1)} %multiply_add_fusion.16), channel_id=1, source_target_pairs={{8,0},{16,8},{24,16},{32,24},{40,32},{48,40},{56,48},{64,56},{72,6... | collective-permute-start | bytes 6152 | tf_op jit(solution)/shard_map/ppermute | solution.py:16
  505.3 7.5 %collective-permute-start.25 = (f32[512]{0:T(512)S(1)}, f32[512]{0:T(512)S(1)}, u32[]{:S(2)}, u32[]{:S(2)}) collective-permute-start(f32[512]{0:T(512)S(1)} %multiply_add_fusion.15), channel_id=1, source_target_pairs={{8,0},{16,8},{24,16},{32,24},{40,32},{48,40},{56,48},{64,56},{72,6... | collective-permute-start | bytes 6152 | tf_op jit(solution)/shard_map/ppermute | solution.py:16
  514.1 7.5 %collective-permute-start.26 = (f32[512]{0:T(512)S(1)}, f32[512]{0:T(512)S(1)}, u32[]{:S(2)}, u32[]{:S(2)}) collective-permute-start(f32[512]{0:T(512)S(1)} %multiply_add_fusion.14), channel_id=1, source_target_pairs={{8,0},{16,8},{24,16},{32,24},{40,32},{48,40},{56,48},{64,56},{72,6... | collective-permute-start | bytes 6152 | tf_op jit(solution)/shard_map/ppermute | solution.py:16
  522.9 7.5 %collective-permute-start.27 = (f32[512]{0:T(512)S(1)}, f32[512]{0:T(512)S(1)}, u32[]{:S(2)}, u32[]{:S(2)}) collective-permute-start(f32[512]{0:T(512)S(1)} %multiply_add_fusion.13), channel_id=1, source_target_pairs={{8,0},{16,8},{24,16},{32,24},{40,32},{48,40},{56,48},{64,56},{72,6... | collective-permute-start | bytes 6152 | tf_op jit(solution)/shard_map/ppermute | solution.py:16
  531.7 7.5 %collective-permute-start.28 = (f32[512]{0:T(512)S(1)}, f32[512]{0:T(512)S(1)}, u32[]{:S(2)}, u32[]{:S(2)}) collective-permute-start(f32[512]{0:T(512)S(1)} %multiply_add_fusion.12), channel_id=1, source_target_pairs={{8,0},{16,8},{24,16},{32,24},{40,32},{48,40},{56,48},{64,56},{72,6... | collective-permute-start | bytes 6152 | tf_op jit(solution)/shard_map/ppermute | solution.py:16
  540.4 7.5 %collective-permute-start.29 = (f32[512]{0:T(512)S(1)}, f32[512]{0:T(512)S(1)}, u32[]{:S(2)}, u32[]{:S(2)}) collective-permute-start(f32[512]{0:T(512)S(1)} %multiply_add_fusion.11), channel_id=1, source_target_pairs={{8,0},{16,8},{24,16},{32,24},{40,32},{48,40},{56,48},{64,56},{72,6... | collective-permute-start | bytes 6152 | tf_op jit(solution)/shard_map/ppermute | solution.py:16
  549.2 7.5 %collective-permute-start.30 = (f32[512]{0:T(512)S(1)}, f32[512]{0:T(512)S(1)}, u32[]{:S(2)}, u32[]{:S(2)}) collective-permute-start(f32[512]{0:T(512)S(1)} %multiply_add_fusion.10), channel_id=1, source_target_pairs={{8,0},{16,8},{24,16},{32,24},{40,32},{48,40},{56,48},{64,56},{72,6... | collective-permute-start | bytes 6152 | tf_op jit(solution)/shard_map/ppermute | solution.py:16
  560.4 6.9 %rev.9 = f32[512,512]{1,0:T(8,128)S(1)} reverse(f32[512,512]{1,0:T(8,128)} %add.413), dimensions={0} | reverse | bytes 2097152 | tf_op jit(solution)/shard_map/rev | solution.py:60
  567.2 5.2 rev.8
  (230 shorter events, 64.4 us)
Async XLA Ops:
  7.2 1.2 copy-start
  7.2 247.7 %all-reduce.38.cloned.1.call-start = ((), (), s32[]{:S(2)}) async-start(), calls=%async_computation | async-start | bytes 2097152 | tf_op jit(solution)/shard_map/psum | solution.py:88
  13.9 5.8 copy-start.2
  166.4 9.0 %copy-start.3 = (f32[3,512,2048]{2,1,0:T(8,128)S(1)}, f32[3,512,2048]{2,1,0:T(8,128)}, u32[]{:S(2)}) copy-start(f32[3,512,2048]{2,1,0:T(8,128)} %copy-done.2) | copy-start | bytes 37748740
  166.5 12.7 %slice-start = ((s8[6291456]{0:T(1024)(128)(4,1)}), s8[4194304]{0:T(1024)(128)(4,1)S(1)}, s32[]{:S(2)}) async-start(s8[6291456]{0:T(1024)(128)(4,1)} %bitcast.57), calls=%async_computation.1 | async-start | bytes 8388608
  175.4 3.7 slice-start.1
  179.1 7.5 %copy-start.4 = (f32[512,512]{1,0:T(8,128)S(1)}, f32[512,512]{1,0:T(8,128)}, u32[]{:S(2)}) copy-start(f32[512,512]{1,0:T(8,128)} %param.9) | copy-start | bytes 3145732
  279.4 5.6 copy-start.5
  288.4 5.8 collective-permute-start
  294.3 8.8 %collective-permute-start.1 = (f32[512]{0:T(512)S(1)}, f32[512]{0:T(512)S(1)}, u32[]{:S(2)}, u32[]{:S(2)}) collective-permute-start(f32[512]{0:T(512)S(1)} %multiply_add_fusion.39), channel_id=1, source_target_pairs={{8,0},{16,8},{24,16},{32,24},{40,32},{48,40},{56,48},{64,56},{72,6... | collective-permute-start | bytes 6152 | tf_op jit(solution)/shard_map/ppermute | solution.py:16
  303.0 8.8 %collective-permute-start.2 = (f32[512]{0:T(512)S(1)}, f32[512]{0:T(512)S(1)}, u32[]{:S(2)}, u32[]{:S(2)}) collective-permute-start(f32[512]{0:T(512)S(1)} %multiply_add_fusion.38), channel_id=1, source_target_pairs={{8,0},{16,8},{24,16},{32,24},{40,32},{48,40},{56,48},{64,56},{72,6... | collective-permute-start | bytes 6152 | tf_op jit(solution)/shard_map/ppermute | solution.py:16
  311.8 8.8 %collective-permute-start.3 = (f32[512]{0:T(512)S(1)}, f32[512]{0:T(512)S(1)}, u32[]{:S(2)}, u32[]{:S(2)}) collective-permute-start(f32[512]{0:T(512)S(1)} %multiply_add_fusion.37), channel_id=1, source_target_pairs={{8,0},{16,8},{24,16},{32,24},{40,32},{48,40},{56,48},{64,56},{72,6... | collective-permute-start | bytes 6152 | tf_op jit(solution)/shard_map/ppermute | solution.py:16
  320.6 8.8 %collective-permute-start.4 = (f32[512]{0:T(512)S(1)}, f32[512]{0:T(512)S(1)}, u32[]{:S(2)}, u32[]{:S(2)}) collective-permute-start(f32[512]{0:T(512)S(1)} %multiply_add_fusion.36), channel_id=1, source_target_pairs={{8,0},{16,8},{24,16},{32,24},{40,32},{48,40},{56,48},{64,56},{72,6... | collective-permute-start | bytes 6152 | tf_op jit(solution)/shard_map/ppermute | solution.py:16
  329.4 8.8 %collective-permute-start.5 = (f32[512]{0:T(512)S(1)}, f32[512]{0:T(512)S(1)}, u32[]{:S(2)}, u32[]{:S(2)}) collective-permute-start(f32[512]{0:T(512)S(1)} %multiply_add_fusion.35), channel_id=1, source_target_pairs={{8,0},{16,8},{24,16},{32,24},{40,32},{48,40},{56,48},{64,56},{72,6... | collective-permute-start | bytes 6152 | tf_op jit(solution)/shard_map/ppermute | solution.py:16
  338.2 8.8 %collective-permute-start.6 = (f32[512]{0:T(512)S(1)}, f32[512]{0:T(512)S(1)}, u32[]{:S(2)}, u32[]{:S(2)}) collective-permute-start(f32[512]{0:T(512)S(1)} %multiply_add_fusion.34), channel_id=1, source_target_pairs={{8,0},{16,8},{24,16},{32,24},{40,32},{48,40},{56,48},{64,56},{72,6... | collective-permute-start | bytes 6152 | tf_op jit(solution)/shard_map/ppermute | solution.py:16
  347.0 8.8 %collective-permute-start.7 = (f32[512]{0:T(512)S(1)}, f32[512]{0:T(512)S(1)}, u32[]{:S(2)}, u32[]{:S(2)}) collective-permute-start(f32[512]{0:T(512)S(1)} %multiply_add_fusion.33), channel_id=1, source_target_pairs={{8,0},{16,8},{24,16},{32,24},{40,32},{48,40},{56,48},{64,56},{72,6... | collective-permute-start | bytes 6152 | tf_op jit(solution)/shard_map/ppermute | solution.py:16
  355.8 8.8 %collective-permute-start.8 = (f32[512]{0:T(512)S(1)}, f32[512]{0:T(512)S(1)}, u32[]{:S(2)}, u32[]{:S(2)}) collective-permute-start(f32[512]{0:T(512)S(1)} %multiply_add_fusion.32), channel_id=1, source_target_pairs={{8,0},{16,8},{24,16},{32,24},{40,32},{48,40},{56,48},{64,56},{72,6... | collective-permute-start | bytes 6152 | tf_op jit(solution)/shard_map/ppermute | solution.py:16
  364.6 8.8 %collective-permute-start.9 = (f32[512]{0:T(512)S(1)}, f32[512]{0:T(512)S(1)}, u32[]{:S(2)}, u32[]{:S(2)}) collective-permute-start(f32[512]{0:T(512)S(1)} %multiply_add_fusion.31), channel_id=1, source_target_pairs={{8,0},{16,8},{24,16},{32,24},{40,32},{48,40},{56,48},{64,56},{72,6... | collective-permute-start | bytes 6152 | tf_op jit(solution)/shard_map/ppermute | solution.py:16
  373.4 8.8 %collective-permute-start.10 = (f32[512]{0:T(512)S(1)}, f32[512]{0:T(512)S(1)}, u32[]{:S(2)}, u32[]{:S(2)}) collective-permute-start(f32[512]{0:T(512)S(1)} %multiply_add_fusion.30), channel_id=1, source_target_pairs={{8,0},{16,8},{24,16},{32,24},{40,32},{48,40},{56,48},{64,56},{72,6... | collective-permute-start | bytes 6152 | tf_op jit(solution)/shard_map/ppermute | solution.py:16
  382.2 8.8 %collective-permute-start.11 = (f32[512]{0:T(512)S(1)}, f32[512]{0:T(512)S(1)}, u32[]{:S(2)}, u32[]{:S(2)}) collective-permute-start(f32[512]{0:T(512)S(1)} %multiply_add_fusion.29), channel_id=1, source_target_pairs={{8,0},{16,8},{24,16},{32,24},{40,32},{48,40},{56,48},{64,56},{72,6... | collective-permute-start | bytes 6152 | tf_op jit(solution)/shard_map/ppermute | solution.py:16
  391.0 8.8 %collective-permute-start.12 = (f32[512]{0:T(512)S(1)}, f32[512]{0:T(512)S(1)}, u32[]{:S(2)}, u32[]{:S(2)}) collective-permute-start(f32[512]{0:T(512)S(1)} %multiply_add_fusion.28), channel_id=1, source_target_pairs={{8,0},{16,8},{24,16},{32,24},{40,32},{48,40},{56,48},{64,56},{72,6... | collective-permute-start | bytes 6152 | tf_op jit(solution)/shard_map/ppermute | solution.py:16
  399.8 8.8 %collective-permute-start.13 = (f32[512]{0:T(512)S(1)}, f32[512]{0:T(512)S(1)}, u32[]{:S(2)}, u32[]{:S(2)}) collective-permute-start(f32[512]{0:T(512)S(1)} %multiply_add_fusion.27), channel_id=1, source_target_pairs={{8,0},{16,8},{24,16},{32,24},{40,32},{48,40},{56,48},{64,56},{72,6... | collective-permute-start | bytes 6152 | tf_op jit(solution)/shard_map/ppermute | solution.py:16
  408.6 8.8 %collective-permute-start.14 = (f32[512]{0:T(512)S(1)}, f32[512]{0:T(512)S(1)}, u32[]{:S(2)}, u32[]{:S(2)}) collective-permute-start(f32[512]{0:T(512)S(1)} %multiply_add_fusion.26), channel_id=1, source_target_pairs={{8,0},{16,8},{24,16},{32,24},{40,32},{48,40},{56,48},{64,56},{72,6... | collective-permute-start | bytes 6152 | tf_op jit(solution)/shard_map/ppermute | solution.py:16
  417.3 8.8 %collective-permute-start.15 = (f32[512]{0:T(512)S(1)}, f32[512]{0:T(512)S(1)}, u32[]{:S(2)}, u32[]{:S(2)}) collective-permute-start(f32[512]{0:T(512)S(1)} %multiply_add_fusion.25), channel_id=1, source_target_pairs={{8,0},{16,8},{24,16},{32,24},{40,32},{48,40},{56,48},{64,56},{72,6... | collective-permute-start | bytes 6152 | tf_op jit(solution)/shard_map/ppermute | solution.py:16
  426.1 8.8 %collective-permute-start.16 = (f32[512]{0:T(512)S(1)}, f32[512]{0:T(512)S(1)}, u32[]{:S(2)}, u32[]{:S(2)}) collective-permute-start(f32[512]{0:T(512)S(1)} %multiply_add_fusion.24), channel_id=1, source_target_pairs={{8,0},{16,8},{24,16},{32,24},{40,32},{48,40},{56,48},{64,56},{72,6... | collective-permute-start | bytes 6152 | tf_op jit(solution)/shard_map/ppermute | solution.py:16
  434.9 8.8 %collective-permute-start.17 = (f32[512]{0:T(512)S(1)}, f32[512]{0:T(512)S(1)}, u32[]{:S(2)}, u32[]{:S(2)}) collective-permute-start(f32[512]{0:T(512)S(1)} %multiply_add_fusion.23), channel_id=1, source_target_pairs={{8,0},{16,8},{24,16},{32,24},{40,32},{48,40},{56,48},{64,56},{72,6... | collective-permute-start | bytes 6152 | tf_op jit(solution)/shard_map/ppermute | solution.py:16
  443.7 8.8 %collective-permute-start.18 = (f32[512]{0:T(512)S(1)}, f32[512]{0:T(512)S(1)}, u32[]{:S(2)}, u32[]{:S(2)}) collective-permute-start(f32[512]{0:T(512)S(1)} %multiply_add_fusion.22), channel_id=1, source_target_pairs={{8,0},{16,8},{24,16},{32,24},{40,32},{48,40},{56,48},{64,56},{72,6... | collective-permute-start | bytes 6152 | tf_op jit(solution)/shard_map/ppermute | solution.py:16
  452.5 8.8 %collective-permute-start.19 = (f32[512]{0:T(512)S(1)}, f32[512]{0:T(512)S(1)}, u32[]{:S(2)}, u32[]{:S(2)}) collective-permute-start(f32[512]{0:T(512)S(1)} %multiply_add_fusion.21), channel_id=1, source_target_pairs={{8,0},{16,8},{24,16},{32,24},{40,32},{48,40},{56,48},{64,56},{72,6... | collective-permute-start | bytes 6152 | tf_op jit(solution)/shard_map/ppermute | solution.py:16
  461.3 8.8 %collective-permute-start.20 = (f32[512]{0:T(512)S(1)}, f32[512]{0:T(512)S(1)}, u32[]{:S(2)}, u32[]{:S(2)}) collective-permute-start(f32[512]{0:T(512)S(1)} %multiply_add_fusion.20), channel_id=1, source_target_pairs={{8,0},{16,8},{24,16},{32,24},{40,32},{48,40},{56,48},{64,56},{72,6... | collective-permute-start | bytes 6152 | tf_op jit(solution)/shard_map/ppermute | solution.py:16
  470.1 8.8 %collective-permute-start.21 = (f32[512]{0:T(512)S(1)}, f32[512]{0:T(512)S(1)}, u32[]{:S(2)}, u32[]{:S(2)}) collective-permute-start(f32[512]{0:T(512)S(1)} %multiply_add_fusion.19), channel_id=1, source_target_pairs={{8,0},{16,8},{24,16},{32,24},{40,32},{48,40},{56,48},{64,56},{72,6... | collective-permute-start | bytes 6152 | tf_op jit(solution)/shard_map/ppermute | solution.py:16
  478.9 8.8 %collective-permute-start.22 = (f32[512]{0:T(512)S(1)}, f32[512]{0:T(512)S(1)}, u32[]{:S(2)}, u32[]{:S(2)}) collective-permute-start(f32[512]{0:T(512)S(1)} %multiply_add_fusion.18), channel_id=1, source_target_pairs={{8,0},{16,8},{24,16},{32,24},{40,32},{48,40},{56,48},{64,56},{72,6... | collective-permute-start | bytes 6152 | tf_op jit(solution)/shard_map/ppermute | solution.py:16
  487.7 8.8 %collective-permute-start.23 = (f32[512]{0:T(512)S(1)}, f32[512]{0:T(512)S(1)}, u32[]{:S(2)}, u32[]{:S(2)}) collective-permute-start(f32[512]{0:T(512)S(1)} %multiply_add_fusion.17), channel_id=1, source_target_pairs={{8,0},{16,8},{24,16},{32,24},{40,32},{48,40},{56,48},{64,56},{72,6... | collective-permute-start | bytes 6152 | tf_op jit(solution)/shard_map/ppermute | solution.py:16
  496.5 8.8 %collective-permute-start.24 = (f32[512]{0:T(512)S(1)}, f32[512]{0:T(512)S(1)}, u32[]{:S(2)}, u32[]{:S(2)}) collective-permute-start(f32[512]{0:T(512)S(1)} %multiply_add_fusion.16), channel_id=1, source_target_pairs={{8,0},{16,8},{24,16},{32,24},{40,32},{48,40},{56,48},{64,56},{72,6... | collective-permute-start | bytes 6152 | tf_op jit(solution)/shard_map/ppermute | solution.py:16
  505.3 8.8 %collective-permute-start.25 = (f32[512]{0:T(512)S(1)}, f32[512]{0:T(512)S(1)}, u32[]{:S(2)}, u32[]{:S(2)}) collective-permute-start(f32[512]{0:T(512)S(1)} %multiply_add_fusion.15), channel_id=1, source_target_pairs={{8,0},{16,8},{24,16},{32,24},{40,32},{48,40},{56,48},{64,56},{72,6... | collective-permute-start | bytes 6152 | tf_op jit(solution)/shard_map/ppermute | solution.py:16
  514.1 8.8 %collective-permute-start.26 = (f32[512]{0:T(512)S(1)}, f32[512]{0:T(512)S(1)}, u32[]{:S(2)}, u32[]{:S(2)}) collective-permute-start(f32[512]{0:T(512)S(1)} %multiply_add_fusion.14), channel_id=1, source_target_pairs={{8,0},{16,8},{24,16},{32,24},{40,32},{48,40},{56,48},{64,56},{72,6... | collective-permute-start | bytes 6152 | tf_op jit(solution)/shard_map/ppermute | solution.py:16
  522.9 8.8 %collective-permute-start.27 = (f32[512]{0:T(512)S(1)}, f32[512]{0:T(512)S(1)}, u32[]{:S(2)}, u32[]{:S(2)}) collective-permute-start(f32[512]{0:T(512)S(1)} %multiply_add_fusion.13), channel_id=1, source_target_pairs={{8,0},{16,8},{24,16},{32,24},{40,32},{48,40},{56,48},{64,56},{72,6... | collective-permute-start | bytes 6152 | tf_op jit(solution)/shard_map/ppermute | solution.py:16
  531.7 8.8 %collective-permute-start.28 = (f32[512]{0:T(512)S(1)}, f32[512]{0:T(512)S(1)}, u32[]{:S(2)}, u32[]{:S(2)}) collective-permute-start(f32[512]{0:T(512)S(1)} %multiply_add_fusion.12), channel_id=1, source_target_pairs={{8,0},{16,8},{24,16},{32,24},{40,32},{48,40},{56,48},{64,56},{72,6... | collective-permute-start | bytes 6152 | tf_op jit(solution)/shard_map/ppermute | solution.py:16
  540.4 8.8 %collective-permute-start.29 = (f32[512]{0:T(512)S(1)}, f32[512]{0:T(512)S(1)}, u32[]{:S(2)}, u32[]{:S(2)}) collective-permute-start(f32[512]{0:T(512)S(1)} %multiply_add_fusion.11), channel_id=1, source_target_pairs={{8,0},{16,8},{24,16},{32,24},{40,32},{48,40},{56,48},{64,56},{72,6... | collective-permute-start | bytes 6152 | tf_op jit(solution)/shard_map/ppermute | solution.py:16
  549.2 23.2 %collective-permute-start.30 = (f32[512]{0:T(512)S(1)}, f32[512]{0:T(512)S(1)}, u32[]{:S(2)}, u32[]{:S(2)}) collective-permute-start(f32[512]{0:T(512)S(1)} %multiply_add_fusion.10), channel_id=1, source_target_pairs={{8,0},{16,8},{24,16},{32,24},{40,32},{48,40},{56,48},{64,56},{72,6... | collective-permute-start | bytes 6152 | tf_op jit(solution)/shard_map/ppermute | solution.py:16
  558.6 16.3 %copy-start.1 = (bf16[512,512]{1,0:T(8,128)(2,1)S(1)}, bf16[512,512]{1,0:T(8,128)(2,1)}, u32[]{:S(2)}) copy-start(bf16[512,512]{1,0:T(8,128)(2,1)} %param.7) | copy-start | bytes 1572868
Sparse Core Ops, SparseCore 0:
  186.8 68.0 all-reduce.37
where the time goes:
time: 588 us; the launch traced here: 582 us
  starting transfers between devices  229 us (39%)
  blocking collectives  144 us (24%)
  waiting for transfers between devices  102 us (17%)
  local copies, waits for them, and re-layouts  47.5 us (8%)
  other arithmetic  30.2 us (5%)
  between operations  15.2 us (3%)
  matrix products  14 us (2%)
    ppermute x31, starting transfers between devices, from_behind(): return lax.ppermute(block, axis, route)  229 us
    pmax x1, blocking collectives, body(): peak_value = lax.pmax(jnp.max(failure_index, axis=0), 'tm')  73 us
    psum x1, blocking collectives, body(): mass_total = lax.psum(jnp.sum(scaled_exp, axis=0), 'tm')  70.8 us
    psum x1, waiting for transfers between devices, body(): load_rows = lax.psum(local_loads, 'elem')  63 us
    ppermute x31, waiting for transfers between devices, from_behind(): return lax.ppermute(block, axis, route)  38.6 us
    slice x66, local copies, waits for them, and re-layouts, chain_back(): lax.associative_scan(compose, (decay_rows, load_rows), reverse=True, axis...  24.4 us
    rev x2, local copies, waits for them, and re-layouts, chain_back(): lax.associative_scan(compose, (decay_rows, load_rows), reverse=True, axis...  12 us
  transfers between devices with their start and end apart: 32, of which 31 were waited for; matrix products, arithmetic and copies ran while one was open for 4% of the time, Pallas kernels for 0%

commit v1 on v0

v1 whole, which is shorter than its diff:
```python
import jax
import jax.numpy as jnp
from jax import lax
from jax.experimental import pallas as pl
from jax.experimental.pallas import tpu as pltpu
from jax.sharding import PartitionSpec as P

MESH = pl.DeviceIdType.MESH
F32 = jnp.float32
BF16 = jnp.bfloat16

NX, NZ, NY = 4, 8, 4
STEPS, MODES, COLS = 512, 512, 2048
LANES = 128
BLOCKS = COLS // LANES
TILE = 256
TILES = COLS // TILE
CHUNKS = 2
CHUNK_TILES = TILES // CHUNKS
CHUNK_COLS = COLS // CHUNKS
CHUNK_BLOCKS = BLOCKS // CHUNKS
SLAB = 64
SLABS = STEPS // SLAB
ROWS = 64
HALF = 32
SHARPNESS = 100.0

NT = (((1,), (1,)), ((), ()))


def kernel(
    modal_hbm, modes_hbm, decay_hbm, layup, lin, quad, base,
    ks_hbm, adjoint_hbm,
    modal, modes, decay, stress_a, stress_b, graded, slab_max, slab_sum, sens, loads,
    pair_in, partial, far_in, near_in, tail_prod, head_prod, offsets, result, ks,
    lse_x, lse_z, carry_x, carry_z, incoming,
    in_sem, out_sem, send_sem, recv_sem,
):
    tm = lax.axis_index("tm")
    elem = lax.axis_index("elem")
    z, x = tm // NX, tm % NX
    y, core = elem // 2, elem % 2
    x_peers = [(z * NX + (x + d) % NX, elem) for d in range(1, NX)]
    z_peers = [(((z + d) % NZ) * NX + x, elem) for d in range(1, NZ)]
    elem_peers = [(tm, (elem + d) % (2 * NY)) for d in range(1, 2 * NY)]
    y_up, y_down, y_far = (y + 1) % NY, (y + 3) % NY, (y + 2) % NY
    up, down, pair = (tm, 2 * y_up + core), (tm, 2 * y_down + core), (tm, 2 * y + 1 - core)

    sent = []
    counter = [0]

    def reserve(count):
        first = counter[0]
        counter[0] += count
        return first

    def send(src, dst, slot, peer):
        copy = pltpu.make_async_remote_copy(
            src_ref=src, dst_ref=dst, send_sem=send_sem.at[slot], recv_sem=recv_sem.at[slot],
            device_id=peer, device_id_type=MESH,
        )
        copy.start()
        sent.append(copy)

    def arrived(dst, slot):
        pltpu.make_async_remote_copy(
            src_ref=dst, dst_ref=dst, send_sem=send_sem.at[slot], recv_sem=recv_sem.at[slot],
            device_id=pair, device_id_type=MESH,
        ).wait_recv()

    modal_copy = pltpu.make_async_copy(modal_hbm, modal, in_sem.at[TILES])
    modal_copy.start()
    tile_copies = []
    for j in range(TILES):
        cols = pl.ds(j * TILE, TILE)
        copy = pltpu.make_async_copy(modes_hbm.at[:, :, cols], modes.at[:, :, cols], in_sem.at[j])
        copy.start()
        tile_copies.append(copy)
    decay_copy = pltpu.make_async_copy(decay_hbm, decay, in_sem.at[TILES + 1])
    decay_copy.start()
    barrier = pltpu.get_barrier_semaphore()
    peers = x_peers + z_peers + elem_peers
    for peer in peers:
        pl.semaphore_signal(barrier, inc=1, device_id=peer, device_id_type=MESH)

    def stress_tile(target, j):
        cols = pl.ds(pl.multiple_of(j * TILE, TILE), TILE)
        for k in range(3):
            target[k] = jnp.dot(modal[...], modes[k, :, cols], preferred_element_type=F32)

    def grade_tile(source, j):
        for h in range(TILE // LANES):
            block = j * (TILE // LANES) + h
            layer = layup[block]
            lin_one = SHARPNESS * lin[0, layer]
            lin_two = SHARPNESS * lin[1, layer]
            quad_one = SHARPNESS * quad[0, layer]
            quad_two = SHARPNESS * quad[1, layer]
            quad_shear = SHARPNESS * quad[2, layer]
            cross = -0.5 * jnp.sqrt(jnp.full((8, LANES), quad_one * quad_two, F32))[None]
            here = pl.ds(h * LANES, LANES)
            there = pl.ds(pl.multiple_of(block * LANES, LANES), LANES)
            for r in range(SLABS):
                rows = pl.ds(r * SLAB, SLAB)
                one, two, shear = (
                    source[k, rows, here].reshape(SLAB // 8, 8, LANES) for k in range(3)
                )
                half_one = quad_one * one + cross * two
                half_two = quad_two * two + cross * one
                half_shear = quad_shear * shear
                slope_one = lin_one + half_one
                slope_two = lin_two + half_two
                index = one * slope_one + two * slope_two + shear * half_shear
                top = jnp.max(index, axis=0)
                mass = jnp.exp(index - top[None])
                slab_max[block, r] = top
                slab_sum[block, r] = jnp.sum(mass, axis=0)
                graded[0, rows, there] = (mass * (slope_one + half_one)).reshape(SLAB, LANES)
                graded[1, rows, there] = (mass * (slope_two + half_two)).reshape(SLAB, LANES)
                graded[2, rows, there] = (mass * half_shear).reshape(SLAB, LANES)

    def stress_pair(p, carry):
        first = 2 * p
        pltpu.make_async_copy(
            modes_hbm.at[:, :, pl.ds(0, TILE)], modes.at[:, :, pl.ds(0, TILE)], in_sem.at[first + 1]
        ).wait()

        @pl.when(first + 2 < TILES)
        def _():
            pltpu.make_async_copy(
                modes_hbm.at[:, :, pl.ds(0, TILE)], modes.at[:, :, pl.ds(0, TILE)], in_sem.at[first + 2]
            ).wait()

        stress_tile(stress_b, first + 1)
        grade_tile(stress_a, first)
        stress_tile(stress_a, jnp.minimum(first + 2, TILES - 1))
        grade_tile(stress_b, first + 1)
        return carry

    lse_x_slot = reserve(CHUNKS * (NX - 1))
    lse_z_slot = reserve(CHUNKS * (NZ - 1))

    def log_sum(values):
        top = jnp.max(values, axis=0)
        return top + jnp.log(jnp.sum(jnp.exp(values - top[None]), axis=0))

    def share_x(c):
        blocks = pl.ds(c * CHUNK_BLOCKS, CHUNK_BLOCKS)
        tops = slab_max[blocks]
        top = jnp.max(tops, axis=(1, 2))
        total = jnp.sum(slab_sum[blocks] * jnp.exp(tops - top[:, None, None, :]), axis=(1, 2))
        lse_x[c, x] = top + jnp.log(total)
        for d, peer in enumerate(x_peers):
            send(lse_x.at[c, x], lse_x.at[c, x], lse_x_slot + c * (NX - 1) + d, peer)

    def share_z(c):
        for d in range(NX - 1):
            arrived(lse_x.at[c, (x + NX - 1 - d) % NX], lse_x_slot + c * (NX - 1) + d)
        lse_z[c, z] = log_sum(lse_x[c])
        for d, peer in enumerate(z_peers):
            send(lse_z.at[c, z], lse_z.at[c, z], lse_z_slot + c * (NZ - 1) + d, peer)

    def finish_lse(c):
        for d in range(NZ - 1):
            arrived(lse_z.at[c, (z + NZ - 1 - d) % NZ], lse_z_slot + c * (NZ - 1) + d)
        lse = log_sum(lse_z[c])
        for b in range(CHUNK_BLOCKS):
            block = c * CHUNK_BLOCKS + b
            ks[pl.ds(block, 1), :] = lse[b : b + 1] * (1.0 / SHARPNESS) + base[layup[block]]
        return lse

    def weigh(c, lse, first_slab, count):
        def slab_step(i, carry):
            r = first_slab + i
            rows = pl.ds(pl.multiple_of(r * SLAB, SLAB), SLAB)
            for b in range(CHUNK_BLOCKS):
                block = c * CHUNK_BLOCKS + b
                scale = jnp.exp(slab_max[block, r] - lse[b : b + 1])[None]
                there = pl.ds(block * LANES, LANES)
                here = pl.ds(b * LANES, LANES)
                for k in range(3):
                    factor = scale if k < 2 else 2.0 * scale
                    value = graded[k, rows, there].reshape(SLAB // 8, 8, LANES) * factor
                    sens[k, rows, here] = value.reshape(SLAB, LANES).astype(BF16)
            return carry

        lax.fori_loop(0, count, slab_step, 0, unroll=True)

    def load_rows(c, half):
        rows = pl.ds(pl.multiple_of(half * (STEPS // 2), STEPS // 2), STEPS // 2)
        total = None
        for k in range(3):
            part = lax.dot_general(
                sens[k, rows, :], modes[k, :, pl.ds(c * CHUNK_COLS, CHUNK_COLS)], NT,
                preferred_element_type=F32,
            )
            total = part if total is None else total + part
        if c == 0:
            loads[rows, :] = total
        else:
            loads[rows, :] += total

    modal_copy.wait()
    tile_copies[0].wait()
    stress_tile(stress_a, 0)
    for c in range(CHUNKS):
        lax.fori_loop(c * CHUNK_TILES // 2, (c + 1) * CHUNK_TILES // 2, stress_pair, 0)
        if c == 0:
            pl.semaphore_wait(barrier, len(peers))
        share_x(c)
    decay_copy.wait()

    ones = tuple(jnp.ones((1, MODES), F32) for _ in range(STEPS // ROWS))

    def tail_step(j, products):
        out = []
        for r in range(STEPS // ROWS):
            row = pl.ds(r * ROWS + ROWS - 1 - j, 1)
            value = products[r] * decay[row, :]
            tail_prod[row, :] = value
            out.append(value)
        return tuple(out)

    def head_step(j, products):
        out = []
        for r in range(STEPS // ROWS):
            row = pl.ds(r * ROWS + j, 1)
            head_prod[row, :] = products[r]
            out.append(products[r] * decay[row, :])
        return tuple(out)

    share_z(0)
    block_prod = lax.fori_loop(0, ROWS, tail_step, ones, unroll=4)
    for c in range(1, CHUNKS):
        share_z(c)
    lax.fori_loop(0, ROWS, head_step, ones, unroll=4)

    for c in range(CHUNKS - 1):
        lse = finish_lse(c)
        weigh(c, lse, 0, SLABS)
        load_rows(c, 0)
        load_rows(c, 1)
    last = CHUNKS - 1
    lse = finish_lse(last)
    ks_copy = pltpu.make_async_copy(ks, ks_hbm, out_sem.at[SLABS])
    ks_copy.start()

    order = (y_far, y_up, y_down, y)
    pair_slot = reserve(4)
    weigh(last, lse, (1 - core) * (SLABS // 2), SLABS // 2)
    load_rows(last, 1 - core)
    for i, q in enumerate(order):
        rows = pl.ds(pl.multiple_of((1 - core) * (STEPS // 2) + q * ROWS, ROWS), ROWS)
        send(loads.at[rows, :], pair_in.at[i], pair_slot + i, pair)
    weigh(last, lse, core * (SLABS // 2), SLABS // 2)
    load_rows(last, core)

    first_half, second_half = pl.ds(0, HALF), pl.ds(HALF, HALF)
    ring_slot = reserve(6)
    for i, q in enumerate(order):
        arrived(pair_in.at[i], pair_slot + i)
        rows = pl.ds(pl.multiple_of(core * (STEPS // 2) + q * ROWS, ROWS), ROWS)
        partial[i] = loads[rows, :] + pair_in[i]
        if i == 0:
            send(partial.at[0, first_half], far_in.at[0], ring_slot, up)
            send(partial.at[0, second_half], far_in.at[1], ring_slot + 1, down)
        if i == 1:
            send(partial.at[1, second_half], near_in.at[0, second_half], ring_slot + 2, up)
        if i == 2:
            send(partial.at[2, first_half], near_in.at[1, first_half], ring_slot + 3, down)

    carry_x_slot = reserve(NX - 1)
    carry_z_slot = reserve(NZ - 1)
    incoming_slot = reserve(2 * NY - 1)
    ahead = jnp.ones((1, MODES), F32)
    state = jnp.zeros((1, MODES), F32)
    for r in range(STEPS // ROWS):
        rows = pl.ds(r * ROWS, ROWS)
        state = state + ahead * jnp.sum(head_prod[rows, :] * loads[rows, :], axis=0, keepdims=True)
        ahead = ahead * block_prod[r]
    carry_x[x, 0:1, :] = ahead
    carry_x[x, 1:2, :] = state
    for d, peer in enumerate(x_peers):
        send(carry_x.at[x], carry_x.at[x], carry_x_slot + d, peer)

    arrived(far_in.at[0], ring_slot)
    partial[1, first_half] = partial[1, first_half] + far_in[0]
    send(partial.at[1, first_half], near_in.at[0, first_half], ring_slot + 4, up)
    arrived(far_in.at[1], ring_slot + 1)
    partial[2, second_half] = partial[2, second_half] + far_in[1]
    send(partial.at[2, second_half], near_in.at[1, second_half], ring_slot + 5, down)

    for d in range(NX - 1):
        arrived(carry_x.at[(x + NX - 1 - d) % NX], carry_x_slot + d)
    slab_scale = jnp.ones((1, MODES), F32)
    slab_state = jnp.zeros((1, MODES), F32)
    later_scale, later_state = slab_scale, slab_state
    for q in range(NX - 1, -1, -1):
        scale, offset = carry_x[q, 0:1, :], carry_x[q, 1:2, :]
        slab_state = offset + scale * slab_state
        slab_scale = scale * slab_scale
        later_state = jnp.where(q > x, offset + scale * later_state, later_state)
        later_scale = jnp.where(q > x, scale * later_scale, later_scale)
    carry_z[z, 0:1, :] = slab_scale
    carry_z[z, 1:2, :] = slab_state
    for d, peer in enumerate(z_peers):
        send(carry_z.at[z], carry_z.at[z], carry_z_slot + d, peer)

    arrived(near_in.at[0, second_half], ring_slot + 2)
    arrived(near_in.at[1, first_half], ring_slot + 3)
    arrived(near_in.at[0, first_half], ring_slot + 4)
    arrived(near_in.at[1, second_half], ring_slot + 5)
    partial[3] = partial[3] + near_in[0] + near_in[1]
    mine = core * NY + y

    def scan_step(j, running):
        row = ROWS - 1 - j
        running = partial[3, pl.ds(row, 1), :] + decay[pl.ds(mine * ROWS + row, 1), :] * running
        offsets[mine, pl.ds(row, 1), :] = running
        return running

    lax.fori_loop(0, ROWS, scan_step, jnp.zeros((1, MODES), F32), unroll=8)

    spread_slot = reserve(6)
    across_slot = reserve(5)

    def spread(block, rows, slot, peer):
        send(offsets.at[block, rows], offsets.at[block, rows], slot, peer)

    whole = pl.ds(0, ROWS)
    spread(mine, first_half, spread_slot, up)
    spread(mine, second_half, spread_slot + 3, down)
    spread(mine, second_half, spread_slot + 1, up)
    spread(mine, first_half, spread_slot + 2, down)
    spread(mine, whole, across_slot, pair)

    for d in range(NZ - 1):
        arrived(carry_z.at[(z + NZ - 1 - d) % NZ], carry_z_slot + d)
    far_state = jnp.zeros((1, MODES), F32)
    for q in range(NZ - 1, -1, -1):
        far_state = jnp.where(q > z, carry_z[q, 1:2, :] + carry_z[q, 0:1, :] * far_state, far_state)
    incoming[elem] = later_state + later_scale * far_state
    for d, peer in enumerate(elem_peers):
        send(incoming.at[elem], incoming.at[elem], incoming_slot + d, peer)

    from_down, from_up, from_far = core * NY + y_down, core * NY + y_up, core * NY + y_far
    arrived(offsets.at[from_down, first_half], spread_slot)
    spread(from_down, first_half, spread_slot + 4, up)
    arrived(offsets.at[from_up, second_half], spread_slot + 3)
    spread(from_up, second_half, spread_slot + 5, down)
    arrived(offsets.at[from_down, second_half], spread_slot + 1)
    spread(from_down, whole, across_slot + 1, pair)
    arrived(offsets.at[from_up, first_half], spread_slot + 2)
    spread(from_up, whole, across_slot + 2, pair)
    arrived(offsets.at[from_far, first_half], spread_slot + 4)
    spread(from_far, first_half, across_slot + 3, pair)
    arrived(offsets.at[from_far, second_half], spread_slot + 5)
    spread(from_far, second_half, across_slot + 4, pair)

    other = (1 - core) * NY
    for d in range(2 * NY - 1):
        arrived(incoming.at[(elem + 2 * NY - 1 - d) % (2 * NY)], incoming_slot + d)
    arrived(offsets.at[other + y], across_slot)
    arrived(offsets.at[other + y_down], across_slot + 1)
    arrived(offsets.at[other + y_up], across_slot + 2)
    arrived(offsets.at[other + y_far, first_half], across_slot + 3)
    arrived(offsets.at[other + y_far, second_half], across_slot + 4)

    behind = incoming[0]
    for e in range(1, 2 * NY):
        behind = behind + incoming[e]
    out_copies = []
    for r in range(SLABS - 1, -1, -1):
        rows = pl.ds(r * ROWS, ROWS)
        result[rows, :] = offsets[r] + tail_prod[rows, :] * behind
        copy = pltpu.make_async_copy(result.at[rows, :], adjoint_hbm.at[rows, :], out_sem.at[r])
        copy.start()
        out_copies.append(copy)
        behind = offsets[r, 0:1, :] + tail_prod[r * ROWS : r * ROWS + 1, :] * behind

    for copy in out_copies:
        copy.wait()
    ks_copy.wait()
    for copy in sent:
        copy.wait_send()


SENDS = CHUNKS * (NX - 1 + NZ - 1) + 4 + 6 + (NX - 1) + (NZ - 1) + (2 * NY - 1) + 6 + 5


def body(modal_coords, stress_modes, step_decay, ply_layup, lin_table, quad_table, base_index):
    smem = pl.BlockSpec(memory_space=pltpu.SMEM)
    hbm = pl.BlockSpec(memory_space=pl.ANY)
    ks, adjoint = pl.pallas_call(
        kernel,
        out_shape=(
            jax.ShapeDtypeStruct((BLOCKS, LANES), F32),
            jax.ShapeDtypeStruct((STEPS, MODES), F32),
        ),
        in_specs=[hbm, hbm, hbm, smem, smem, smem, smem],
        out_specs=(hbm, hbm),
        scratch_shapes=[
            pltpu.VMEM((STEPS, MODES), BF16),
            pltpu.VMEM((3, MODES, COLS), BF16),
            pltpu.VMEM((STEPS, MODES), F32),
            pltpu.VMEM((3, STEPS, TILE), F32),
            pltpu.VMEM((3, STEPS, TILE), F32),
            pltpu.VMEM((3, STEPS, COLS), F32),
            pltpu.VMEM((BLOCKS, SLABS, 8, LANES), F32),
            pltpu.VMEM((BLOCKS, SLABS, 8, LANES), F32),
            pltpu.VMEM((3, STEPS, CHUNK_COLS), BF16),
            pltpu.VMEM((STEPS, MODES), F32),
            pltpu.VMEM((4, ROWS, MODES), F32),
            pltpu.VMEM((4, ROWS, MODES), F32),
            pltpu.VMEM((2, HALF, MODES), F32),
            pltpu.VMEM((2, ROWS, MODES), F32),
            pltpu.VMEM((STEPS, MODES), F32),
            pltpu.VMEM((STEPS, MODES), F32),
            pltpu.VMEM((2 * NY, ROWS, MODES), F32),
            pltpu.VMEM((STEPS, MODES), F32),
            pltpu.VMEM((BLOCKS, LANES), F32),
            pltpu.VMEM((CHUNKS, NX, CHUNK_BLOCKS, LANES), F32),
            pltpu.VMEM((CHUNKS, NZ, CHUNK_BLOCKS, LANES), F32),
            pltpu.VMEM((NX, 2, MODES), F32),
            pltpu.VMEM((NZ, 2, MODES), F32),
            pltpu.VMEM((2 * NY, 1, MODES), F32),
            pltpu.SemaphoreType.DMA((TILES + 2,)),
            pltpu.SemaphoreType.DMA((SLABS + 1,)),
            pltpu.SemaphoreType.DMA((SENDS,)),
            pltpu.SemaphoreType.DMA((SENDS,)),
        ],
        compiler_params=pltpu.CompilerParams(
            collective_id=0, has_side_effects=True, vmem_limit_bytes=60 * 1024 * 1024
        ),
        name="gust_adjoint",
    )(
        modal_coords, stress_modes, step_decay, ply_layup,
        lin_table.T, quad_table.T, base_index,
    )
    return ks.reshape(COLS), adjoint


def solution(mesh):
    return jax.shard_map(
        body,
        mesh=mesh,
        in_specs=(P("tm", None), P(None, None, "elem"), P("tm", None), P("elem"), P(), P(), P()),
        out_specs=(P("elem"), P("tm", None)),
        check_vma=False,
    )
```

time: 588 us -> 51.3 us (0.09)
  the two profiles are of different devices: /device:TPU:128 before, /device:TPU:1 now
where the time goes in v1:
time: 51.3 us; the launch traced here: 50.9 us
  Pallas kernels  46.7 us (91%)
  local copies, waits for them, and re-layouts  3.56 us (7%)
  between operations  0.64 us (1%)
    pallas_call x1, Pallas kernels, body(): pl.pallas_call(kernel, out_shape=(jax.ShapeDtypeStruct((BLOCKS, LANES), F...  46.7 us
    unnamed x2, local copies, waits for them, and re-layouts  3.56 us

profile of v1, /device:TPU:1, one launch (start us, length us, event | category | flops | bytes accessed | tf_op | source)
XLA Modules:
  0.0 50.9 jit_solution(14533420473313274806)
XLA Ops:
  0.6 46.7 %gust_adjoint.1 = (f32[16,128]{1,0:T(8,128)}, f32[512,512]{1,0:T(8,128)}) custom-call(bf16[512,512]{1,0:T(8,128)(2,1)} %modal_hbm.1, bf16[3,512,2048]{2,1,0:T(8,128)(2,1)} %modes_hbm.1, f32[512,512]{1,0:T(8,128)} %decay_hbm.1, s32[16]{0:T(128)} %layup.1, f32[2,16]{1,0:T(2,128)} %bitcast.5, f32[3,16]{1,0:T(4,128)} %bitcast.4, f32[16]{0:T(128)} %base.1), custom_call_target="tpu_custom_call" | custom-call | tf_op jit(solution)/shard_map/gust_adjoint/pallas_call | solution.py:394
  47.4 1.3 %copy.11 = f32[2048]{0:T(1024)} copy(f32[2048]{0:T(1024)} %bitcast.3) | data formatting | bytes 16384
  48.7 2.3 %copy.12 = f32[512,512]{1,0:T(8,128)} copy(f32[512,512]{1,0:T(8,128)} %get-tuple-element.9) | data formatting | bytes 2097152

commit v2 on v1

v2 whole, which is shorter than its diff:
```python
import math

import jax
import jax.numpy as jnp
from jax import lax
from jax.experimental import pallas as pl
from jax.experimental.pallas import tpu as pltpu
from jax.sharding import PartitionSpec as P

MESH = pl.DeviceIdType.MESH
F32 = jnp.float32
BF16 = jnp.bfloat16

NX, NZ, NY = 4, 8, 4
STEPS, MODES, COLS = 512, 512, 2048
LANES = 128
GROUPS = MODES // LANES
BLOCKS = COLS // LANES
LAYUPS = 16
TILE = 256
TILES = COLS // TILE
CHUNKS = TILES // 2
CHUNK_COLS = COLS // CHUNKS
CHUNK_BLOCKS = BLOCKS // CHUNKS
SLAB = 64
SLABS = STEPS // SLAB
ROWS = 64
ROW_BLOCKS = STEPS // ROWS
HALF = 32
PIECES = 2
WIDTH = MODES // PIECES
SHARPNESS = 100.0
SCALE = SHARPNESS * math.log2(math.e)
SHIFT = -math.log2(math.log(2.0))

NT = (((1,), (1,)), ((), ()))

LSE_X = 0
LSE_Z = LSE_X + CHUNKS * (NX - 1)
PAIR = LSE_Z + CHUNKS * (NZ - 1)
RING = PAIR + 4 * PIECES
CARRY_X = RING + 6 * PIECES
CARRY_Z = CARRY_X + NX - 1
INCOMING = CARRY_Z + NZ - 1
SPREAD = INCOMING + 2 * NY - 1
ACROSS = SPREAD + 6 * PIECES
SENDS = ACROSS + 5 * PIECES

MODAL_IN = TILES
DECAY_IN = TILES + 1
TABLE_IN = DECAY_IN + GROUPS
INPUTS = TABLE_IN + 4


def kernel(
    modal_hbm, modes_hbm, decay_hbm, layup_hbm, lin_hbm, quad_hbm, base_hbm,
    ks, result,
    layup, lin, quad, base,
    modal, modes, decay, stress_a, stress_b, graded, slab_max, slab_sum, sens, loads,
    pair_in, partial, far_in, near_in, tail_prod, head_prod, offsets,
    lse_x, lse_z, carry_x, carry_z, incoming,
    in_sem, send_sem, recv_sem,
):
    tm = lax.axis_index("tm")
    elem = lax.axis_index("elem")
    z, x = tm // NX, tm % NX
    y, core = elem // 2, elem % 2
    x_peers = [(z * NX + (x + d) % NX, elem) for d in range(1, NX)]
    z_peers = [(((z + d) % NZ) * NX + x, elem) for d in range(1, NZ)]
    elem_peers = [(tm, (elem + d) % (2 * NY)) for d in range(1, 2 * NY)]
    y_up, y_down, y_far = (y + 1) % NY, (y + 3) % NY, (y + 2) % NY
    up, down, pair = (tm, 2 * y_up + core), (tm, 2 * y_down + core), (tm, 2 * y + 1 - core)

    sent = []

    def describe(src, dst, slot, peer):
        return pltpu.make_async_remote_copy(
            src_ref=src, dst_ref=dst, send_sem=send_sem.at[slot], recv_sem=recv_sem.at[slot],
            device_id=peer, device_id_type=MESH,
        )

    def send(src, dst, slot, peer):
        copy = describe(src, dst, slot, peer)
        copy.start()
        sent.append(copy)

    def arrived(dst, slot):
        describe(dst, dst, slot, pair).wait_recv()

    table_copies = [
        pltpu.make_async_copy(src, dst, in_sem.at[TABLE_IN + i])
        for i, (src, dst) in enumerate(
            ((layup_hbm, layup), (lin_hbm, lin), (quad_hbm, quad), (base_hbm, base))
        )
    ]

    def tile_copy(j):
        cols = pl.ds(j * TILE, TILE)
        return pltpu.make_async_copy(modes_hbm.at[:, :, cols], modes.at[:, :, cols], in_sem.at[j])

    modal_copy = pltpu.make_async_copy(modal_hbm, modal, in_sem.at[MODAL_IN])
    modal_copy.start()
    tile_copy(0).start()
    for copy in table_copies:
        copy.start()
    for j in range(1, TILES):
        tile_copy(j).start()
    decay_copies = []
    for g in range(GROUPS):
        copy = pltpu.make_async_copy(
            decay_hbm.at[:, pl.ds(g * LANES, LANES)], decay.at[g], in_sem.at[DECAY_IN + g]
        )
        copy.start()
        decay_copies.append(copy)
    barrier = pltpu.get_barrier_semaphore()
    peers = x_peers + z_peers + elem_peers
    for peer in peers:
        pl.semaphore_signal(barrier, inc=1, device_id=peer, device_id_type=MESH)

    def stress_tile(target, j):
        cols = pl.ds(pl.multiple_of(j * TILE, TILE), TILE)
        for k in range(3):
            target[k] = jnp.dot(modal[...], modes[k, :, cols], preferred_element_type=F32)

    def grade_tile(source, j):
        for h in range(TILE // LANES):
            block = j * (TILE // LANES) + h
            layer = layup[block]
            lin_one = SCALE * lin[0, layer]
            lin_two = SCALE * lin[1, layer]
            quad_one = SCALE * quad[0, layer]
            quad_two = SCALE * quad[1, layer]
            quad_shear = SCALE * quad[2, layer]
            cross = -0.5 * jnp.sqrt(jnp.full((8, LANES), quad_one * quad_two, F32))[None]
            here = pl.ds(h * LANES, LANES)
            there = pl.ds(pl.multiple_of(block * LANES, LANES), LANES)
            for r in range(SLABS):
                rows = pl.ds(r * SLAB, SLAB)
                one, two, shear = (
                    source[k, rows, here].reshape(SLAB // 8, 8, LANES) for k in range(3)
                )
                half_one = quad_one * one + cross * two
                half_two = quad_two * two + cross * one
                half_shear = quad_shear * shear
                slope_one = lin_one + half_one
                slope_two = lin_two + half_two
                index = one * slope_one + two * slope_two + shear * half_shear
                top = jnp.max(index, axis=0)
                mass = jnp.exp2(index - top[None])
                slab_max[block, r] = top
                slab_sum[block, r] = jnp.sum(mass, axis=0)
                graded[0, rows, there] = (mass * (slope_one + half_one)).reshape(SLAB, LANES)
                graded[1, rows, there] = (mass * (slope_two + half_two)).reshape(SLAB, LANES)
                graded[2, rows, there] = (mass * half_shear).reshape(SLAB, LANES)

    def log_two(values):
        return jnp.log(values) * math.log2(math.e)

    def log_sum(values):
        top = jnp.max(values, axis=0)
        return top + log_two(jnp.sum(jnp.exp2(values - top[None]), axis=0))

    def share_x(c):
        blocks = pl.ds(c * CHUNK_BLOCKS, CHUNK_BLOCKS)
        tops = slab_max[blocks]
        top = jnp.max(tops, axis=(1, 2))
        total = jnp.sum(slab_sum[blocks] * jnp.exp2(tops - top[:, None, None, :]), axis=(1, 2))
        lse_x[c, x] = top + log_two(total)
        for d, peer in enumerate(x_peers):
            describe(lse_x.at[c, x], lse_x.at[c, x], LSE_X + c * (NX - 1) + d, peer).start()

    def share_z(c):
        for d in range(NX - 1):
            arrived(lse_x.at[c, (x + NX - 1 - d) % NX], LSE_X + c * (NX - 1) + d)
        lse_z[c, z] = log_sum(lse_x[c])
        for d, peer in enumerate(z_peers):
            describe(lse_z.at[c, z], lse_z.at[c, z], LSE_Z + c * (NZ - 1) + d, peer).start()

    def finish_lse(c):
        for d in range(NZ - 1):
            arrived(lse_z.at[c, (z + NZ - 1 - d) % NZ], LSE_Z + c * (NZ - 1) + d)
        lse = log_sum(lse_z[c])
        for b in range(CHUNK_BLOCKS):
            block = c * CHUNK_BLOCKS + b
            ks[pl.ds(block, 1), :] = lse[b : b + 1] * (1.0 / SCALE) + base[layup[block]]
        return lse + SHIFT

    def weigh(c, lse, half):
        for i in range(SLABS // 2):
            r = half * (SLABS // 2) + i
            rows = pl.ds(pl.multiple_of(r * SLAB, SLAB), SLAB)
            for b in range(CHUNK_BLOCKS):
                block = c * CHUNK_BLOCKS + b
                scale = jnp.exp2(slab_max[block, r] - lse[b : b + 1])[None]
                there = pl.ds(block * LANES, LANES)
                here = pl.ds(b * LANES, LANES)
                for k in range(3):
                    factor = scale if k < 2 else 2.0 * scale
                    value = graded[k, rows, there].reshape(SLAB // 8, 8, LANES) * factor
                    sens[k, rows, here] = value.reshape(SLAB, LANES).astype(BF16)

    def load_rows(c, half, piece):
        rows = pl.ds(pl.multiple_of(half * (STEPS // 2), STEPS // 2), STEPS // 2)
        total = None
        for k in range(3):
            part = lax.dot_general(
                sens[k, rows, :],
                modes[k, pl.ds(piece * WIDTH, WIDTH), pl.ds(c * CHUNK_COLS, CHUNK_COLS)],
                NT, preferred_element_type=F32,
            )
            total = part if total is None else total + part
        if c == 0:
            loads[piece, rows, :] = total
        else:
            loads[piece, rows, :] += total

    modal_copy.wait()
    tile_copy(0).wait()
    stress_tile(stress_a, 0)
    for copy in table_copies:
        copy.wait()

    def stress_chunk(c, carry):
        first = 2 * c
        tile_copy(first + 1).wait()

        @pl.when(first + 2 < TILES)
        def _():
            tile_copy(first + 2).wait()

        stress_tile(stress_b, first + 1)
        grade_tile(stress_a, first)
        stress_tile(stress_a, jnp.minimum(first + 2, TILES - 1))
        grade_tile(stress_b, first + 1)

        @pl.when(c == 0)
        def _():
            pl.semaphore_wait(barrier, len(peers))

        share_x(c)

        @pl.when(c >= 2)
        def _():
            share_z(c - 2)

        return carry

    lax.fori_loop(0, CHUNKS, stress_chunk, 0)

    for copy in decay_copies:
        copy.wait()
    ones = tuple(jnp.ones((ROW_BLOCKS, LANES), F32) for _ in range(2 * GROUPS))

    def product_step(j, products):
        tails, heads = [], []
        for g in range(GROUPS):
            rows = pl.ds(ROWS - 1 - j, ROW_BLOCKS, stride=ROWS)
            value = products[g] * decay[g, rows, :]
            tail_prod[g, rows, :] = value
            tails.append(value)
            rows = pl.ds(j, ROW_BLOCKS, stride=ROWS)
            value = products[GROUPS + g]
            head_prod[g, rows, :] = value
            heads.append(value * decay[g, rows, :])
        return tuple(tails + heads)

    block_prod = lax.fori_loop(0, ROWS, product_step, ones, unroll=8)[:GROUPS]

    share_z(CHUNKS - 2)
    for c in range(CHUNKS - 1):
        lse = finish_lse(c)
        for half in range(2):
            weigh(c, lse, half)
            for piece in range(PIECES):
                load_rows(c, half, piece)
        if c == 0:
            share_z(CHUNKS - 1)
    last = CHUNKS - 1
    lse = finish_lse(last)

    order = (y_far, y_up, y_down, y)
    weigh(last, lse, 1 - core)
    for piece in range(PIECES):
        load_rows(last, 1 - core, piece)
        for i, q in enumerate(order):
            rows = pl.ds(pl.multiple_of((1 - core) * (STEPS // 2) + q * ROWS, ROWS), ROWS)
            send(loads.at[piece, rows, :], pair_in.at[piece, i], PAIR + 4 * piece + i, pair)
    weigh(last, lse, core)
    for piece in range(PIECES):
        load_rows(last, core, piece)

    first_half, second_half = pl.ds(0, HALF), pl.ds(HALF, HALF)
    for piece in range(PIECES):
        slot = RING + 6 * piece
        for i, q in enumerate(order):
            arrived(pair_in.at[piece, i], PAIR + 4 * piece + i)
            rows = pl.ds(pl.multiple_of(core * (STEPS // 2) + q * ROWS, ROWS), ROWS)
            partial[piece, i] = loads[piece, rows, :] + pair_in[piece, i]
            if i == 0:
                send(partial.at[piece, 0, first_half], far_in.at[piece, 0], slot, up)
                send(partial.at[piece, 0, second_half], far_in.at[piece, 1], slot + 1, down)
            if i == 1:
                send(
                    partial.at[piece, 1, second_half], near_in.at[piece, 0, second_half],
                    slot + 2, up,
                )
            if i == 2:
                send(
                    partial.at[piece, 2, first_half], near_in.at[piece, 1, first_half],
                    slot + 3, down,
                )

    for g in range(GROUPS):
        piece, lanes = g // 2, pl.ds((g % 2) * LANES, LANES)
        ahead = jnp.ones((1, LANES), F32)
        state = jnp.zeros((1, LANES), F32)
        for r in range(ROW_BLOCKS):
            rows = pl.ds(r * ROWS, ROWS)
            block_sum = jnp.sum(head_prod[g, rows, :] * loads[piece, rows, lanes], axis=0, keepdims=True)
            state = state + ahead * block_sum
            ahead = ahead * block_prod[g][r : r + 1]
        carry_x[x, 0:1, pl.ds(g * LANES, LANES)] = ahead
        carry_x[x, 1:2, pl.ds(g * LANES, LANES)] = state
    for d, peer in enumerate(x_peers):
        send(carry_x.at[x], carry_x.at[x], CARRY_X + d, peer)

    for piece in range(PIECES):
        slot = RING + 6 * piece
        arrived(far_in.at[piece, 0], slot)
        partial[piece, 1, first_half] = partial[piece, 1, first_half] + far_in[piece, 0]
        send(partial.at[piece, 1, first_half], near_in.at[piece, 0, first_half], slot + 4, up)
        arrived(far_in.at[piece, 1], slot + 1)
        partial[piece, 2, second_half] = partial[piece, 2, second_half] + far_in[piece, 1]
        send(partial.at[piece, 2, second_half], near_in.at[piece, 1, second_half], slot + 5, down)

    for d in range(NX - 1):
        arrived(carry_x.at[(x + NX - 1 - d) % NX], CARRY_X + d)
    slab_scale = jnp.ones((1, MODES), F32)
    slab_state = jnp.zeros((1, MODES), F32)
    later_scale, later_state = slab_scale, slab_state
    for q in range(NX - 1, -1, -1):
        scale, offset = carry_x[q, 0:1, :], carry_x[q, 1:2, :]
        slab_state = offset + scale * slab_state
        slab_scale = scale * slab_scale
        later_state = jnp.where(q > x, offset + scale * later_state, later_state)
        later_scale = jnp.where(q > x, scale * later_scale, later_scale)
    carry_z[z, 0:1, :] = slab_scale
    carry_z[z, 1:2, :] = slab_state
    for d, peer in enumerate(z_peers):
        send(carry_z.at[z], carry_z.at[z], CARRY_Z + d, peer)

    mine = core * NY + y

    def spread(piece, block, rows, slot, peer):
        send(offsets.at[piece, block, rows], offsets.at[piece, block, rows], slot, peer)

    whole = pl.ds(0, ROWS)
    for piece in range(PIECES):
        slot = RING + 6 * piece
        arrived(near_in.at[piece, 0, second_half], slot + 2)
        arrived(near_in.at[piece, 1, first_half], slot + 3)
        arrived(near_in.at[piece, 0, first_half], slot + 4)
        arrived(near_in.at[piece, 1, second_half], slot + 5)
        partial[piece, 3] = partial[piece, 3] + near_in[piece, 0] + near_in[piece, 1]
        running = [jnp.zeros((1, LANES), F32) for _ in range(2)]
        for row in range(ROWS - 1, -1, -1):
            for h in range(2):
                lanes = pl.ds(h * LANES, LANES)
                factor = decay[2 * piece + h, pl.ds(mine * ROWS + row, 1), :]
                running[h] = partial[piece, 3, row : row + 1, lanes] + factor * running[h]
                offsets[piece, mine, row : row + 1, lanes] = running[h]
        slot = SPREAD + 6 * piece
        spread(piece, mine, first_half, slot, up)
        spread(piece, mine, second_half, slot + 3, down)
        spread(piece, mine, second_half, slot + 1, up)
        spread(piece, mine, first_half, slot + 2, down)
        spread(piece, mine, whole, ACROSS + 5 * piece, pair)

    for d in range(NZ - 1):
        arrived(carry_z.at[(z + NZ - 1 - d) % NZ], CARRY_Z + d)
    far_state = jnp.zeros((1, MODES), F32)
    for q in range(NZ - 1, -1, -1):
        far_state = jnp.where(q > z, carry_z[q, 1:2, :] + carry_z[q, 0:1, :] * far_state, far_state)
    incoming[elem] = later_state + later_scale * far_state
    for d, peer in enumerate(elem_peers):
        send(incoming.at[elem], incoming.at[elem], INCOMING + d, peer)

    from_down, from_up, from_far = core * NY + y_down, core * NY + y_up, core * NY + y_far
    for piece in range(PIECES):
        slot, across = SPREAD + 6 * piece, ACROSS + 5 * piece
        arrived(offsets.at[piece, from_down, first_half], slot)
        spread(piece, from_down, first_half, slot + 4, up)
        arrived(offsets.at[piece, from_up, second_half], slot + 3)
        spread(piece, from_up, second_half, slot + 5, down)
        arrived(offsets.at[piece, from_down, second_half], slot + 1)
        spread(piece, from_down, whole, across + 1, pair)
        arrived(offsets.at[piece, from_up, first_half], slot + 2)
        spread(piece, from_up, whole, across + 2, pair)
    for piece in range(PIECES):
        slot, across = SPREAD + 6 * piece, ACROSS + 5 * piece
        arrived(offsets.at[piece, from_far, first_half], slot + 4)
        spread(piece, from_far, first_half, across + 3, pair)
        arrived(offsets.at[piece, from_far, second_half], slot + 5)
        spread(piece, from_far, second_half, across + 4, pair)

    for d in range(2 * NY - 1):
        arrived(incoming.at[(elem + 2 * NY - 1 - d) % (2 * NY)], INCOMING + d)
    behind = incoming[0]
    for e in range(1, 2 * NY):
        behind = behind + incoming[e]

    other = (1 - core) * NY
    for piece in range(PIECES):
        across = ACROSS + 5 * piece
        arrived(offsets.at[piece, other + y], across)
        arrived(offsets.at[piece, other + y_down], across + 1)
        arrived(offsets.at[piece, other + y_up], across + 2)
        arrived(offsets.at[piece, other + y_far, first_half], across + 3)
        arrived(offsets.at[piece, other + y_far, second_half], across + 4)
        for h in range(2):
            g = 2 * piece + h
            here, there = pl.ds(h * LANES, LANES), pl.ds(g * LANES, LANES)
            state = behind[:, g * LANES : (g + 1) * LANES]
            for r in range(ROW_BLOCKS - 1, -1, -1):
                rows = pl.ds(r * ROWS, ROWS)
                result[rows, there] = offsets[piece, r, :, here] + tail_prod[g, rows, :] * state
                state = offsets[piece, r, 0:1, here] + tail_prod[g, r * ROWS : r * ROWS + 1, :] * state

    for copy in sent:
        copy.wait_send()
    for c in range(CHUNKS):
        for d, peer in enumerate(x_peers):
            describe(lse_x.at[c, x], lse_x.at[c, x], LSE_X + c * (NX - 1) + d, peer).wait_send()
        for d, peer in enumerate(z_peers):
            describe(lse_z.at[c, z], lse_z.at[c, z], LSE_Z + c * (NZ - 1) + d, peer).wait_send()


def write_out(ks, result, ks_hbm, adjoint_hbm, sem):
    copies = [
        pltpu.make_async_copy(result, adjoint_hbm, sem.at[0]),
        pltpu.make_async_copy(ks, ks_hbm, sem.at[1]),
    ]
    for copy in copies:
        copy.start()
    for copy in copies:
        copy.wait()


def body(modal_coords, stress_modes, step_decay, ply_layup, lin_table, quad_table, base_index):
    hbm = pl.BlockSpec(memory_space=pl.ANY)
    vmem = pl.BlockSpec(memory_space=pltpu.VMEM)
    ks, adjoint = pl.pallas_call(
        kernel,
        out_shape=(
            pltpu.VMEM((BLOCKS, LANES), F32),
            pltpu.VMEM((STEPS, MODES), F32),
        ),
        in_specs=[hbm] * 7,
        out_specs=(vmem, vmem),
        scratch_shapes=[
            pltpu.SMEM((BLOCKS,), jnp.int32),
            pltpu.SMEM((2, LAYUPS), F32),
            pltpu.SMEM((3, LAYUPS), F32),
            pltpu.SMEM((LAYUPS,), F32),
            pltpu.VMEM((STEPS, MODES), BF16),
            pltpu.VMEM((3, MODES, COLS), BF16),
            pltpu.VMEM((GROUPS, STEPS, LANES), F32),
            pltpu.VMEM((3, STEPS, TILE), F32),
            pltpu.VMEM((3, STEPS, TILE), F32),
            pltpu.VMEM((3, STEPS, COLS), F32),
            pltpu.VMEM((BLOCKS, SLABS, 8, LANES), F32),
            pltpu.VMEM((BLOCKS, SLABS, 8, LANES), F32),
            pltpu.VMEM((3, STEPS, CHUNK_COLS), BF16),
            pltpu.VMEM((PIECES, STEPS, WIDTH), F32),
            pltpu.VMEM((PIECES, 4, ROWS, WIDTH), F32),
            pltpu.VMEM((PIECES, 4, ROWS, WIDTH), F32),
            pltpu.VMEM((PIECES, 2, HALF, WIDTH), F32),
            pltpu.VMEM((PIECES, 2, ROWS, WIDTH), F32),
            pltpu.VMEM((GROUPS, STEPS, LANES), F32),
            pltpu.VMEM((GROUPS, STEPS, LANES), F32),
            pltpu.VMEM((PIECES, ROW_BLOCKS, ROWS, WIDTH), F32),
            pltpu.VMEM((CHUNKS, NX, CHUNK_BLOCKS, LANES), F32),
            pltpu.VMEM((CHUNKS, NZ, CHUNK_BLOCKS, LANES), F32),
            pltpu.VMEM((NX, 2, MODES), F32),
            pltpu.VMEM((NZ, 2, MODES), F32),
            pltpu.VMEM((2 * NY, 1, MODES), F32),
            pltpu.SemaphoreType.DMA((INPUTS,)),
            pltpu.SemaphoreType.DMA((SENDS,)),
            pltpu.SemaphoreType.DMA((SENDS,)),
        ],
        compiler_params=pltpu.CompilerParams(
            collective_id=0, has_side_effects=True, vmem_limit_bytes=48 * 1024 * 1024
        ),
        name="gust_adjoint",
    )(*(
        pltpu.with_memory_space_constraint(value, pltpu.HBM)
        for value in (
            modal_coords, stress_modes, step_decay, ply_layup,
            lin_table.T, quad_table.T, base_index,
        )
    ))
    ks, adjoint = pl.pallas_call(
        write_out,
        out_shape=(
            jax.ShapeDtypeStruct((BLOCKS, LANES), F32),
            jax.ShapeDtypeStruct((STEPS, MODES), F32),
        ),
        in_specs=[vmem] * 2,
        out_specs=(hbm, hbm),
        scratch_shapes=[pltpu.SemaphoreType.DMA((2,))],
        name="write_out",
    )(
        pltpu.with_memory_space_constraint(ks, pltpu.VMEM),
        pltpu.with_memory_space_constraint(adjoint, pltpu.VMEM),
    )
    return ks.reshape(COLS), adjoint


def solution(mesh):
    return jax.shard_map(
        body,
        mesh=mesh,
        in_specs=(P("tm", None), P(None, None, "elem"), P("tm", None), P("elem"), P(), P(), P()),
        out_specs=(P("elem"), P("tm", None)),
        check_vma=False,
    )
```

time: 51.3 us -> 47.5 us (0.926)
  local copies, waits for them, and re-layouts: 3.56 us -> 0 us
    unnamed x2 -> x0, local copies, waits for them, and re-layouts: 3.56 us -> none
    pallas_call x1 -> x2, Pallas kernels: 46.7 us -> 46.6 us  [the longest x1 45.6 us: body(): pl.pallas_call(kernel, out_shape=(pltpu.VMEM((BLOCKS, LANES), F32), pltpu...]
where the time goes in v2:
time: 47.5 us; the launch traced here: 47.2 us
  Pallas kernels  46.6 us (98%)
  between operations  0.64 us (1%)
    pallas_call x1, Pallas kernels, body(): pl.pallas_call(kernel, out_shape=(pltpu.VMEM((BLOCKS, LANES), F32), pltpu...  45.6 us
    pallas_call x1, Pallas kernels, body(): pl.pallas_call(write_out, out_shape=(jax.ShapeDtypeStruct((BLOCKS, LANES)...  0.99 us

profile of v2, /device:TPU:1, one launch (start us, length us, event | category | flops | bytes accessed | tf_op | source)
XLA Modules:
  0.0 47.2 jit_solution(782254552797419162)
XLA Ops:
  0.6 45.6 %gust_adjoint.1 = (f32[16,128]{1,0:T(8,128)S(1)}, f32[512,512]{1,0:T(8,128)S(1)}) custom-call(bf16[512,512]{1,0:T(8,128)(2,1)} %modal_hbm.1, bf16[3,512,2048]{2,1,0:T(8,128)(2,1)} %modes_hbm.1, f32[512,512]{1,0:T(8,128)} %decay_hbm.1, s32[16]{0:T(128)} %layup_hbm.1, f32[2,16]{1,0:T(2,128)} %bitcast.4, f32[3,16]{1,0:T(4,128)} %bitcast.3, f32[16]{0:T(128)} %base_hbm.1), custom_call_target="tpu_custom_call" | custom-call | tf_op jit(solution)/shard_map/gust_adjoint/pallas_call | solution.py:452
  46.2 1.0 %write_out.1 = (f32[16,128]{1,0:T(8,128)}, f32[512,512]{1,0:T(8,128)}) custom-call(f32[16,128]{1,0:T(8,128)S(1)} %get-tuple-element.6.ks, f32[512,512]{1,0:T(8,128)S(1)} %get-tuple-element.7.result), custom_call_target="tpu_custom_call" | custom-call | tf_op jit(solution)/shard_map/write_out/pallas_call | solution.py:502

commit v3 on v2

v3 whole, which is shorter than its diff:
```python
import math

import jax
import jax.numpy as jnp
from jax import lax
from jax.experimental import pallas as pl
from jax.experimental.pallas import tpu as pltpu
from jax.sharding import PartitionSpec as P

MESH = pl.DeviceIdType.MESH
F32 = jnp.float32
BF16 = jnp.bfloat16

NX, NZ, NY = 4, 8, 4
STEPS, MODES, COLS = 512, 512, 2048
LANES = 128
GROUPS = MODES // LANES
BLOCKS = COLS // LANES
LAYUPS = 16
TILE = 256
TILES = COLS // TILE
CHUNKS = TILES // 2
CHUNK_COLS = COLS // CHUNKS
CHUNK_BLOCKS = BLOCKS // CHUNKS
SLAB = 64
SLABS = STEPS // SLAB
ROWS = 64
ROW_BLOCKS = STEPS // ROWS
WIDTH = 256
PER_DOT = WIDTH // LANES
SHARPNESS = 100.0
SCALE = SHARPNESS * math.log2(math.e)
HALF_SCALE = 0.5 * SCALE
SHIFT = -math.log2(2.0 * math.log(2.0))

NT = (((1,), (1,)), ((), ()))

LSE_X = 0
LSE_Z = LSE_X + CHUNKS * (NX - 1)
PAIR = LSE_Z + CHUNKS * (NZ - 1)
RING = PAIR + GROUPS
CARRY_X = RING + (NY - 1) * GROUPS
CARRY_Z = CARRY_X + NX - 1
INCOMING = CARRY_Z + NZ - 1
SPREAD = INCOMING + 2 * NY - 1
ACROSS = SPREAD + (NY - 1) * GROUPS
SENDS = ACROSS + NY * GROUPS

MODAL_IN = TILES
DECAY_IN = TILES + 1
TABLE_IN = DECAY_IN + GROUPS
INPUTS = TABLE_IN + 4


def kernel(
    modal_hbm, modes_hbm, decay_hbm, layup_hbm, lin_hbm, quad_hbm, base_hbm,
    ks, result,
    layup, lin, quad, base,
    modal, modes, decay, stress_a, stress_b, graded, index, slab_max, block_max, block_sum, sens, loads,
    pair_in, partial, near_in, tail_prod, head_prod, offsets,
    lse_x, lse_z, carry_x, carry_z, incoming,
    in_sem, send_sem, recv_sem,
):
    tm = lax.axis_index("tm")
    elem = lax.axis_index("elem")
    z, x = tm // NX, tm % NX
    y, core = elem // 2, elem % 2
    x_peers = [(z * NX + (x + d) % NX, elem) for d in range(1, NX)]
    z_peers = [(((z + d) % NZ) * NX + x, elem) for d in range(1, NZ)]
    elem_peers = [(tm, (elem + d) % (2 * NY)) for d in range(1, 2 * NY)]
    y_up, y_down, y_far = (y + 1) % NY, (y + 3) % NY, (y + 2) % NY
    pair = (tm, 2 * y + 1 - core)
    ring = [(tm, 2 * q + core) for q in (y_far, y_up, y_down)]
    ring_y = (y_far, y_down, y_up)

    sent = []

    def describe(src, dst, slot, peer):
        return pltpu.make_async_remote_copy(
            src_ref=src, dst_ref=dst, send_sem=send_sem.at[slot], recv_sem=recv_sem.at[slot],
            device_id=peer, device_id_type=MESH,
        )

    def send(src, dst, slot, peer):
        copy = describe(src, dst, slot, peer)
        copy.start()
        sent.append(copy)

    def arrived(dst, slot):
        describe(dst, dst, slot, pair).wait_recv()

    table_copies = [
        pltpu.make_async_copy(src, dst, in_sem.at[TABLE_IN + i])
        for i, (src, dst) in enumerate(
            ((layup_hbm, layup), (lin_hbm, lin), (quad_hbm, quad), (base_hbm, base))
        )
    ]

    def tile_copy(j):
        cols = pl.ds(j * TILE, TILE)
        return pltpu.make_async_copy(modes_hbm.at[:, :, cols], modes.at[:, :, cols], in_sem.at[j])

    modal_copy = pltpu.make_async_copy(modal_hbm, modal, in_sem.at[MODAL_IN])
    modal_copy.start()
    tile_copy(0).start()
    for copy in table_copies:
        copy.start()
    for j in range(1, TILES):
        tile_copy(j).start()
    decay_copies = []
    for g in range(GROUPS):
        copy = pltpu.make_async_copy(
            decay_hbm.at[:, pl.ds(g * LANES, LANES)], decay.at[g], in_sem.at[DECAY_IN + g]
        )
        copy.start()
        decay_copies.append(copy)
    barrier = pltpu.get_barrier_semaphore()
    peers = x_peers + z_peers + elem_peers
    for peer in peers:
        pl.semaphore_signal(barrier, inc=1, device_id=peer, device_id_type=MESH)

    def stress_tile(target, j):
        cols = pl.ds(pl.multiple_of(j * TILE, TILE), TILE)
        for k in range(3):
            target[k] = jnp.dot(modal[...], modes[k, :, cols], preferred_element_type=F32)

    def grade_tile(source, j):
        for h in range(TILE // LANES):
            block = j * (TILE // LANES) + h
            layer = layup[block]
            lin_one = HALF_SCALE * lin[0, layer]
            lin_two = HALF_SCALE * lin[1, layer]
            quad_one = SCALE * quad[0, layer]
            quad_two = SCALE * quad[1, layer]
            quad_shear = SCALE * quad[2, layer]
            cross = -0.5 * jnp.sqrt(jnp.full((8, LANES), quad_one * quad_two, F32))[None]
            here = pl.ds(h * LANES, LANES)
            there = pl.ds(pl.multiple_of(block * LANES, LANES), LANES)
            for r in range(SLABS):
                rows = pl.ds(r * SLAB, SLAB)
                one, two, shear = (
                    source[k, rows, here].reshape(SLAB // 8, 8, LANES) for k in range(3)
                )
                slope_one = lin_one + (quad_one * one + cross * two)
                slope_two = lin_two + (quad_two * two + cross * one)
                slope_shear = quad_shear * shear
                value = (
                    one * (lin_one + slope_one) + two * (lin_two + slope_two) + shear * slope_shear
                )
                graded[0, rows, there] = slope_one.reshape(SLAB, LANES)
                graded[1, rows, there] = slope_two.reshape(SLAB, LANES)
                graded[2, rows, there] = slope_shear.reshape(SLAB, LANES)
                index[rows, there] = value.reshape(SLAB, LANES)
                slab_max[block, r] = jnp.max(value, axis=0)

    def sum_tile(j):
        for h in range(TILE // LANES):
            block = j * (TILE // LANES) + h
            there = pl.ds(pl.multiple_of(block * LANES, LANES), LANES)
            top = jnp.max(slab_max[block], axis=0)
            parts = []
            for r in range(SLABS):
                value = index[pl.ds(r * SLAB, SLAB), there].reshape(SLAB // 8, 8, LANES)
                parts.append(jnp.sum(jnp.exp2(value - top[None]), axis=0))
            while len(parts) > 1:
                parts = [a + b for a, b in zip(parts[::2], parts[1::2])]
            block_max[block] = top
            block_sum[block] = parts[0]

    def log_two(values):
        return jnp.log(values) * math.log2(math.e)

    def log_sum(values):
        top = jnp.max(values, axis=0)
        return top + log_two(jnp.sum(jnp.exp2(values - top[None]), axis=0))

    def share_x(c):
        blocks = pl.ds(c * CHUNK_BLOCKS, CHUNK_BLOCKS)
        tops = block_max[blocks]
        top = jnp.max(tops, axis=1)
        total = jnp.sum(block_sum[blocks] * jnp.exp2(tops - top[:, None, :]), axis=1)
        lse_x[c, x] = top + log_two(total)
        for d, peer in enumerate(x_peers):
            describe(lse_x.at[c, x], lse_x.at[c, x], LSE_X + c * (NX - 1) + d, peer).start()

    def share_z(c):
        for d in range(NX - 1):
            arrived(lse_x.at[c, (x + NX - 1 - d) % NX], LSE_X + c * (NX - 1) + d)
        lse_z[c, z] = log_sum(lse_x[c])
        for d, peer in enumerate(z_peers):
            describe(lse_z.at[c, z], lse_z.at[c, z], LSE_Z + c * (NZ - 1) + d, peer).start()

    def finish_lse(c):
        for d in range(NZ - 1):
            arrived(lse_z.at[c, (z + NZ - 1 - d) % NZ], LSE_Z + c * (NZ - 1) + d)
        lse = log_sum(lse_z[c])
        for b in range(CHUNK_BLOCKS):
            block = c * CHUNK_BLOCKS + b
            ks[pl.ds(block, 1), :] = lse[b : b + 1] * (1.0 / SCALE) + base[layup[block]]
        return lse + SHIFT

    def weigh(c, lse, half):
        for i in range(SLABS // 2):
            r = half * (SLABS // 2) + i
            rows = pl.ds(pl.multiple_of(r * SLAB, SLAB), SLAB)
            for b in range(CHUNK_BLOCKS):
                there = pl.ds((c * CHUNK_BLOCKS + b) * LANES, LANES)
                here = pl.ds(b * LANES, LANES)
                weight = jnp.exp2(index[rows, there] - lse[b : b + 1])
                for k in range(3):
                    sens[k, rows, here] = (weight * graded[k, rows, there]).astype(BF16)

    def load_rows(c, half, piece):
        rows = pl.ds(pl.multiple_of(half * (STEPS // 2), STEPS // 2), STEPS // 2)
        total = None
        for k in range(3):
            part = lax.dot_general(
                sens[k, rows, :],
                modes[k, pl.ds(piece * WIDTH, WIDTH), pl.ds(c * CHUNK_COLS, CHUNK_COLS)],
                NT, preferred_element_type=F32,
            )
            total = part if total is None else total + part
        for h in range(PER_DOT):
            g = piece * PER_DOT + h
            part = total[:, h * LANES : (h + 1) * LANES]
            loads[g, rows, :] = part if c == 0 else loads[g, rows, :] + part

    modal_copy.wait()
    tile_copy(0).wait()
    stress_tile(stress_a, 0)
    for copy in table_copies:
        copy.wait()

    def stress_chunk(c, carry):
        first = 2 * c
        tile_copy(first + 1).wait()
        stress_tile(stress_b, first + 1)
        grade_tile(stress_a, first)

        @pl.when(first + 2 < TILES)
        def _():
            tile_copy(first + 2).wait()

        stress_tile(stress_a, jnp.minimum(first + 2, TILES - 1))
        grade_tile(stress_b, first + 1)
        sum_tile(first)

        @pl.when(c == 0)
        def _():
            pl.semaphore_wait(barrier, len(peers))

        sum_tile(first + 1)
        share_x(c)

        @pl.when(c >= 2)
        def _():
            share_z(c - 2)

        return carry

    lax.fori_loop(0, CHUNKS, stress_chunk, 0)

    for copy in decay_copies:
        copy.wait()
    tiles = ROWS // 8
    level = lax.broadcasted_iota(jnp.int32, (tiles, 8, LANES), 1)

    def product_step(i, carry):
        g, r = i // ROW_BLOCKS, i % ROW_BLOCKS
        rows = pl.ds(pl.multiple_of(r * ROWS, ROWS), ROWS)
        tail = decay[g, rows, :].reshape(tiles, 8, LANES)
        head = tail
        for step in (1, 2, 4):
            tail = tail * jnp.where(level < 8 - step, pltpu.roll(tail, 8 - step, 1), 1.0)
            head = head * jnp.where(level >= step, pltpu.roll(head, step, 1), 1.0)
        before = jnp.where(level >= 1, pltpu.roll(head, 1, 1), 1.0)
        after = jnp.ones((1, LANES), F32)
        ahead = jnp.ones((1, LANES), F32)
        for n in range(tiles):
            m = tiles - 1 - n
            tail_prod[g, pl.ds(pl.multiple_of(r * ROWS + m * 8, 8), 8), :] = tail[m] * after
            after = after * tail[m, 0:1]
            head_prod[g, pl.ds(pl.multiple_of(r * ROWS + n * 8, 8), 8), :] = before[n] * ahead
            ahead = ahead * head[n, 7:8]
        return carry

    lax.fori_loop(0, GROUPS * ROW_BLOCKS, product_step, 0, unroll=4)

    share_z(CHUNKS - 2)
    for c in range(CHUNKS - 1):
        lse = finish_lse(c)
        for half in range(2):
            weigh(c, lse, half)
            for piece in range(MODES // WIDTH):
                load_rows(c, half, piece)
        if c == 0:
            share_z(CHUNKS - 1)
    last = CHUNKS - 1
    lse = finish_lse(last)

    pair_rows = pl.ds(pl.multiple_of((1 - core) * (STEPS // 2), STEPS // 2), STEPS // 2)
    weigh(last, lse, 1 - core)
    for piece in range(MODES // WIDTH):
        load_rows(last, 1 - core, piece)
        for g in range(piece * PER_DOT, (piece + 1) * PER_DOT):
            send(loads.at[g, pair_rows, :], pair_in.at[g], PAIR + g, pair)
    weigh(last, lse, core)
    for piece in range(MODES // WIDTH):
        load_rows(last, core, piece)

    def pair_sum(g, q):
        here = pl.ds(pl.multiple_of(q * ROWS, ROWS), ROWS)
        there = pl.ds(pl.multiple_of(core * (STEPS // 2) + q * ROWS, ROWS), ROWS)
        return loads[g, there, :] + pair_in[g, here, :]

    for g in range(GROUPS):
        arrived(pair_in.at[g], PAIR + g)
        for i, q in enumerate((y_far, y_up, y_down)):
            partial[g, i] = pair_sum(g, q)
            send(partial.at[g, i], near_in.at[g, i], RING + (NY - 1) * g + i, ring[i])

    for g in range(GROUPS):
        ahead = jnp.ones((1, LANES), F32)
        state = jnp.zeros((1, LANES), F32)
        for r in range(ROW_BLOCKS):
            rows = pl.ds(r * ROWS, ROWS)
            block_sum = jnp.sum(head_prod[g, rows, :] * loads[g, rows, :], axis=0, keepdims=True)
            state = state + ahead * block_sum
            ahead = ahead * tail_prod[g, r * ROWS : r * ROWS + 1, :]
        carry_x[x, 0:1, pl.ds(g * LANES, LANES)] = ahead
        carry_x[x, 1:2, pl.ds(g * LANES, LANES)] = state
    for d, peer in enumerate(x_peers):
        send(carry_x.at[x], carry_x.at[x], CARRY_X + d, peer)

    for d in range(NX - 1):
        arrived(carry_x.at[(x + NX - 1 - d) % NX], CARRY_X + d)
    slab_scale = jnp.ones((1, MODES), F32)
    slab_state = jnp.zeros((1, MODES), F32)
    later_scale, later_state = slab_scale, slab_state
    for q in range(NX - 1, -1, -1):
        scale, offset = carry_x[q, 0:1, :], carry_x[q, 1:2, :]
        slab_state = offset + scale * slab_state
        slab_scale = scale * slab_scale
        later_state = jnp.where(q > x, offset + scale * later_state, later_state)
        later_scale = jnp.where(q > x, scale * later_scale, later_scale)
    carry_z[z, 0:1, :] = slab_scale
    carry_z[z, 1:2, :] = slab_state
    for d, peer in enumerate(z_peers):
        send(carry_z.at[z], carry_z.at[z], CARRY_Z + d, peer)

    mine = core * NY + y

    def spread(g, block, slot, peer):
        send(offsets.at[g, block], offsets.at[g, block], slot, peer)

    mine_rows = pl.ds(pl.multiple_of(mine * ROWS, ROWS), ROWS)
    for g in range(GROUPS):
        for i in range(NY - 1):
            arrived(near_in.at[g, i], RING + (NY - 1) * g + i)
        state = (pair_sum(g, y) + near_in[g, 1]) + (near_in[g, 2] + near_in[g, 0])
        state = state.reshape(tiles, 8, LANES)
        factor = decay[g, mine_rows, :].reshape(tiles, 8, LANES)
        for step in (1, 2, 4):
            inside = level < 8 - step
            state = state + factor * jnp.where(inside, pltpu.roll(state, 8 - step, 1), 0.0)
            factor = factor * jnp.where(inside, pltpu.roll(factor, 8 - step, 1), 1.0)
        running = jnp.zeros((1, LANES), F32)
        for m in range(tiles - 1, -1, -1):
            value = state[m] + factor[m] * running
            offsets[g, mine, pl.ds(m * 8, 8), :] = value
            running = value[0:1]
        for i in range(NY - 1):
            spread(g, mine, SPREAD + (NY - 1) * g + i, ring[i])
        spread(g, mine, ACROSS + NY * g, pair)

    for d in range(NZ - 1):
        arrived(carry_z.at[(z + NZ - 1 - d) % NZ], CARRY_Z + d)
    far_state = jnp.zeros((1, MODES), F32)
    for q in range(NZ - 1, -1, -1):
        far_state = jnp.where(q > z, carry_z[q, 1:2, :] + carry_z[q, 0:1, :] * far_state, far_state)
    incoming[elem] = later_state + later_scale * far_state
    for d, peer in enumerate(elem_peers):
        send(incoming.at[elem], incoming.at[elem], INCOMING + d, peer)

    for g in range(GROUPS):
        for i, q in enumerate(ring_y):
            arrived(offsets.at[g, core * NY + q], SPREAD + (NY - 1) * g + i)
            spread(g, core * NY + q, ACROSS + NY * g + 1 + i, pair)

    for d in range(2 * NY - 1):
        arrived(incoming.at[(elem + 2 * NY - 1 - d) % (2 * NY)], INCOMING + d)
    behind = incoming[0]
    for e in range(1, 2 * NY):
        behind = behind + incoming[e]

    other = (1 - core) * NY
    for g in range(GROUPS):
        for i, q in enumerate((y,) + ring_y):
            arrived(offsets.at[g, other + q], ACROSS + NY * g + i)
        there = pl.ds(g * LANES, LANES)
        state = behind[:, g * LANES : (g + 1) * LANES]
        for r in range(ROW_BLOCKS - 1, -1, -1):
            rows = pl.ds(r * ROWS, ROWS)
            result[rows, there] = offsets[g, r] + tail_prod[g, rows, :] * state
            state = offsets[g, r, 0:1, :] + tail_prod[g, r * ROWS : r * ROWS + 1, :] * state

    for copy in sent:
        copy.wait_send()
    for c in range(CHUNKS):
        for d, peer in enumerate(x_peers):
            describe(lse_x.at[c, x], lse_x.at[c, x], LSE_X + c * (NX - 1) + d, peer).wait_send()
        for d, peer in enumerate(z_peers):
            describe(lse_z.at[c, z], lse_z.at[c, z], LSE_Z + c * (NZ - 1) + d, peer).wait_send()


def write_out(ks, result, ks_hbm, adjoint_hbm, sem):
    copies = [
        pltpu.make_async_copy(result, adjoint_hbm, sem.at[0]),
        pltpu.make_async_copy(ks, ks_hbm, sem.at[1]),
    ]
    for copy in copies:
        copy.start()
    for copy in copies:
        copy.wait()


def body(modal_coords, stress_modes, step_decay, ply_layup, lin_table, quad_table, base_index):
    hbm = pl.BlockSpec(memory_space=pl.ANY)
    vmem = pl.BlockSpec(memory_space=pltpu.VMEM)
    ks, adjoint = pl.pallas_call(
        kernel,
        out_shape=(
            pltpu.VMEM((BLOCKS, LANES), F32),
            pltpu.VMEM((STEPS, MODES), F32),
        ),
        in_specs=[hbm] * 7,
        out_specs=(vmem, vmem),
        scratch_shapes=[
            pltpu.SMEM((BLOCKS,), jnp.int32),
            pltpu.SMEM((2, LAYUPS), F32),
            pltpu.SMEM((3, LAYUPS), F32),
            pltpu.SMEM((LAYUPS,), F32),
            pltpu.VMEM((STEPS, MODES), BF16),
            pltpu.VMEM((3, MODES, COLS), BF16),
            pltpu.VMEM((GROUPS, STEPS, LANES), F32),
            pltpu.VMEM((3, STEPS, TILE), F32),
            pltpu.VMEM((3, STEPS, TILE), F32),
            pltpu.VMEM((3, STEPS, COLS), F32),
            pltpu.VMEM((STEPS, COLS), F32),
            pltpu.VMEM((BLOCKS, SLABS, 8, LANES), F32),
            pltpu.VMEM((BLOCKS, 8, LANES), F32),
            pltpu.VMEM((BLOCKS, 8, LANES), F32),
            pltpu.VMEM((3, STEPS, CHUNK_COLS), BF16),
            pltpu.VMEM((GROUPS, STEPS, LANES), F32),
            pltpu.VMEM((GROUPS, STEPS // 2, LANES), F32),
            pltpu.VMEM((GROUPS, NY - 1, ROWS, LANES), F32),
            pltpu.VMEM((GROUPS, NY - 1, ROWS, LANES), F32),
            pltpu.VMEM((GROUPS, STEPS, LANES), F32),
            pltpu.VMEM((GROUPS, STEPS, LANES), F32),
            pltpu.VMEM((GROUPS, ROW_BLOCKS, ROWS, LANES), F32),
            pltpu.VMEM((CHUNKS, NX, CHUNK_BLOCKS, LANES), F32),
            pltpu.VMEM((CHUNKS, NZ, CHUNK_BLOCKS, LANES), F32),
            pltpu.VMEM((NX, 2, MODES), F32),
            pltpu.VMEM((NZ, 2, MODES), F32),
            pltpu.VMEM((2 * NY, 1, MODES), F32),
            pltpu.SemaphoreType.DMA((INPUTS,)),
            pltpu.SemaphoreType.DMA((SENDS,)),
            pltpu.SemaphoreType.DMA((SENDS,)),
        ],
        compiler_params=pltpu.CompilerParams(
            collective_id=0, has_side_effects=True, vmem_limit_bytes=48 * 1024 * 1024
        ),
        name="gust_adjoint",
    )(*(
        pltpu.with_memory_space_constraint(value, pltpu.HBM)
        for value in (
            modal_coords, stress_modes, step_decay, ply_layup,
            lin_table.T, quad_table.T, base_index,
        )
    ))
    ks, adjoint = pl.pallas_call(
        write_out,
        out_shape=(
            jax.ShapeDtypeStruct((BLOCKS, LANES), F32),
            jax.ShapeDtypeStruct((STEPS, MODES), F32),
        ),
        in_specs=[vmem] * 2,
        out_specs=(hbm, hbm),
        scratch_shapes=[pltpu.SemaphoreType.DMA((2,))],
        name="write_out",
    )(
        pltpu.with_memory_space_constraint(ks, pltpu.VMEM),
        pltpu.with_memory_space_constraint(adjoint, pltpu.VMEM),
    )
    return ks.reshape(COLS), adjoint


def solution(mesh):
    return jax.shard_map(
        body,
        mesh=mesh,
        in_specs=(P("tm", None), P(None, None, "elem"), P("tm", None), P("elem"), P(), P(), P()),
        out_specs=(P("elem"), P("tm", None)),
        check_vma=False,
    )
```

time: 47.5 us -> 48.3 us (1.017)
  Pallas kernels: 46.6 us -> 47.5 us
    pallas_call x1, Pallas kernels: 45.6 us -> 46.5 us  [body(): pl.pallas_call(kernel, out_shape=(pltpu.VMEM((BLOCKS, LANES), F32), pltpu...]
where the time goes in v3:
time: 48.3 us; the launch traced here: 48.2 us
  Pallas kernels  47.5 us (98%)
  between operations  0.64 us (1%)
    pallas_call x1, Pallas kernels, body(): pl.pallas_call(kernel, out_shape=(pltpu.VMEM((BLOCKS, LANES), F32), pltpu...  46.5 us
    pallas_call x1, Pallas kernels, body(): pl.pallas_call(write_out, out_shape=(jax.ShapeDtypeStruct((BLOCKS, LANES)...  0.99 us

profile of v3, /device:TPU:1, one launch (start us, length us, event | category | flops | bytes accessed | tf_op | source)
XLA Modules:
  0.0 48.2 jit_solution(9207571200034355770)
XLA Ops:
  0.6 46.5 %gust_adjoint.1 = (f32[16,128]{1,0:T(8,128)S(1)}, f32[512,512]{1,0:T(8,128)S(1)}) custom-call(bf16[512,512]{1,0:T(8,128)(2,1)} %modal_hbm.1, bf16[3,512,2048]{2,1,0:T(8,128)(2,1)} %modes_hbm.1, f32[512,512]{1,0:T(8,128)} %decay_hbm.1, s32[16]{0:T(128)} %layup_hbm.1, f32[2,16]{1,0:T(2,128)} %bitcast.4, f32[3,16]{1,0:T(4,128)} %bitcast.3, f32[16]{0:T(128)} %base_hbm.1), custom_call_target="tpu_custom_call" | custom-call | tf_op jit(solution)/shard_map/gust_adjoint/pallas_call | solution.py:430
  47.2 1.0 %write_out.1 = (f32[16,128]{1,0:T(8,128)}, f32[512,512]{1,0:T(8,128)}) custom-call(f32[16,128]{1,0:T(8,128)S(1)} %get-tuple-element.6.ks, f32[512,512]{1,0:T(8,128)S(1)} %get-tuple-element.7.result), custom_call_target="tpu_custom_call" | custom-call | tf_op jit(solution)/shard_map/write_out/pallas_call | solution.py:481

commit v4 on v3

--- a/solution.py
+++ b/solution.py
@@ -18,8 +18,10 @@
 BLOCKS = COLS // LANES
 LAYUPS = 16
 TILE = 256
+PARTS = 1
+PART = STEPS // PARTS
 TILES = COLS // TILE
-CHUNKS = TILES // 2
+CHUNKS = 2
 CHUNK_COLS = COLS // CHUNKS
 CHUNK_BLOCKS = BLOCKS // CHUNKS
 SLAB = 64
@@ -35,9 +37,8 @@
 
 NT = (((1,), (1,)), ((), ()))
 
-LSE_X = 0
-LSE_Z = LSE_X + CHUNKS * (NX - 1)
-PAIR = LSE_Z + CHUNKS * (NZ - 1)
+LSE = 0
+PAIR = LSE + CHUNKS * (NX * NZ - 1)
 RING = PAIR + GROUPS
 CARRY_X = RING + (NY - 1) * GROUPS
 CARRY_Z = CARRY_X + NX - 1
@@ -56,9 +57,9 @@
     modal_hbm, modes_hbm, decay_hbm, layup_hbm, lin_hbm, quad_hbm, base_hbm,
     ks, result,
     layup, lin, quad, base,
-    modal, modes, decay, stress_a, stress_b, graded, index, slab_max, block_max, block_sum, sens, loads,
+    modal, modes, decay, stress, graded, index, slab_max, block_max, block_sum, sens, loads,
     pair_in, partial, near_in, tail_prod, head_prod, offsets,
-    lse_x, lse_z, carry_x, carry_z, incoming,
+    shares, carry_x, carry_z, incoming,
     in_sem, send_sem, recv_sem,
 ):
     tm = lax.axis_index("tm")
@@ -67,6 +68,10 @@
     y, core = elem // 2, elem % 2
     x_peers = [(z * NX + (x + d) % NX, elem) for d in range(1, NX)]
     z_peers = [(((z + d) % NZ) * NX + x, elem) for d in range(1, NZ)]
+    offsets_zx = sorted(
+        ((dz, dx) for dz in range(NZ) for dx in range(NX) if dz or dx),
+        key=lambda o: -min(o[0], NZ - o[0]) - min(o[1], NX - o[1]),
+    )
     elem_peers = [(tm, (elem + d) % (2 * NY)) for d in range(1, 2 * NY)]
     y_up, y_down, y_far = (y + 1) % NY, (y + 3) % NY, (y + 2) % NY
     pair = (tm, 2 * y + 1 - core)
@@ -115,16 +120,20 @@
         copy.start()
         decay_copies.append(copy)
     barrier = pltpu.get_barrier_semaphore()
-    peers = x_peers + z_peers + elem_peers
+    peers = elem_peers + [
+        (((z + dz) % NZ) * NX + (x + dx) % NX, elem) for dz, dx in offsets_zx
+    ]
     for peer in peers:
         pl.semaphore_signal(barrier, inc=1, device_id=peer, device_id_type=MESH)
 
-    def stress_tile(target, j):
+    def stress_part(target, j, part):
         cols = pl.ds(pl.multiple_of(j * TILE, TILE), TILE)
         for k in range(3):
-            target[k] = jnp.dot(modal[...], modes[k, :, cols], preferred_element_type=F32)
-
-    def grade_tile(source, j):
+            target[k] = jnp.dot(
+                modal[pl.ds(part * PART, PART), :], modes[k, :, cols], preferred_element_type=F32
+            )
+
+    def grade_part(source, j, part):
         for h in range(TILE // LANES):
             block = j * (TILE // LANES) + h
             layer = layup[block]
@@ -136,10 +145,11 @@
             cross = -0.5 * jnp.sqrt(jnp.full((8, LANES), quad_one * quad_two, F32))[None]
             here = pl.ds(h * LANES, LANES)
             there = pl.ds(pl.multiple_of(block * LANES, LANES), LANES)
-            for r in range(SLABS):
+            for r in range(part * SLABS // PARTS, (part + 1) * SLABS // PARTS):
                 rows = pl.ds(r * SLAB, SLAB)
+                inner = pl.ds(r * SLAB - part * PART, SLAB)
                 one, two, shear = (
-                    source[k, rows, here].reshape(SLAB // 8, 8, LANES) for k in range(3)
+                    source[k, inner, here].reshape(SLAB // 8, 8, LANES) for k in range(3)
                 )
                 slope_one = lin_one + (quad_one * one + cross * two)
                 slope_two = lin_two + (quad_two * two + cross * one)
@@ -174,26 +184,25 @@
         top = jnp.max(values, axis=0)
         return top + log_two(jnp.sum(jnp.exp2(values - top[None]), axis=0))
 
-    def share_x(c):
+    def share_copies(c):
+        for d, (dz, dx) in enumerate(offsets_zx):
+            peer = (((z + dz) % NZ) * NX + (x + dx) % NX, elem)
+            yield describe(shares.at[c, tm], shares.at[c, tm], LSE + c * (NX * NZ - 1) + d, peer)
+
+    def share(c):
         blocks = pl.ds(c * CHUNK_BLOCKS, CHUNK_BLOCKS)
         tops = block_max[blocks]
         top = jnp.max(tops, axis=1)
         total = jnp.sum(block_sum[blocks] * jnp.exp2(tops - top[:, None, :]), axis=1)
-        lse_x[c, x] = top + log_two(total)
-        for d, peer in enumerate(x_peers):
-            describe(lse_x.at[c, x], lse_x.at[c, x], LSE_X + c * (NX - 1) + d, peer).start()
-
-    def share_z(c):
-        for d in range(NX - 1):
-            arrived(lse_x.at[c, (x + NX - 1 - d) % NX], LSE_X + c * (NX - 1) + d)
-        lse_z[c, z] = log_sum(lse_x[c])
-        for d, peer in enumerate(z_peers):
-            describe(lse_z.at[c, z], lse_z.at[c, z], LSE_Z + c * (NZ - 1) + d, peer).start()
+        shares[c, tm] = top + log_two(total)
+        for copy in share_copies(c):
+            copy.start()
 
     def finish_lse(c):
-        for d in range(NZ - 1):
-            arrived(lse_z.at[c, (z + NZ - 1 - d) % NZ], LSE_Z + c * (NZ - 1) + d)
-        lse = log_sum(lse_z[c])
+        for d, (dz, dx) in enumerate(offsets_zx):
+            source = ((z + NZ - dz) % NZ) * NX + (x + NX - dx) % NX
+            arrived(shares.at[c, source], LSE + c * (NX * NZ - 1) + d)
+        lse = log_sum(shares[c])
         for b in range(CHUNK_BLOCKS):
             block = c * CHUNK_BLOCKS + b
             ks[pl.ds(block, 1), :] = lse[b : b + 1] * (1.0 / SCALE) + base[layup[block]]
@@ -226,39 +235,33 @@
             loads[g, rows, :] = part if c == 0 else loads[g, rows, :] + part
 
     modal_copy.wait()
-    tile_copy(0).wait()
-    stress_tile(stress_a, 0)
     for copy in table_copies:
         copy.wait()
 
-    def stress_chunk(c, carry):
-        first = 2 * c
+    def stress_pair(p, carry):
+        first = 2 * p
+        tile_copy(first).wait()
         tile_copy(first + 1).wait()
-        stress_tile(stress_b, first + 1)
-        grade_tile(stress_a, first)
-
-        @pl.when(first + 2 < TILES)
-        def _():
-            tile_copy(first + 2).wait()
-
-        stress_tile(stress_a, jnp.minimum(first + 2, TILES - 1))
-        grade_tile(stress_b, first + 1)
+        for n in range(2):
+            for part in range(PARTS):
+                target = stress.at[n * PARTS + part]
+                stress_part(target, first + n, part)
+                grade_part(target, first + n, part)
         sum_tile(first)
 
-        @pl.when(c == 0)
+        @pl.when(p == 0)
         def _():
             pl.semaphore_wait(barrier, len(peers))
 
         sum_tile(first + 1)
-        share_x(c)
-
-        @pl.when(c >= 2)
+
+        @pl.when(p % 2 == 1)
         def _():
-            share_z(c - 2)
+            share(p // 2)
 
         return carry
 
-    lax.fori_loop(0, CHUNKS, stress_chunk, 0)
+    lax.fori_loop(0, TILES // 2, stress_pair, 0)
 
     for copy in decay_copies:
         copy.wait()
@@ -286,15 +289,12 @@
 
     lax.fori_loop(0, GROUPS * ROW_BLOCKS, product_step, 0, unroll=4)
 
-    share_z(CHUNKS - 2)
     for c in range(CHUNKS - 1):
         lse = finish_lse(c)
         for half in range(2):
             weigh(c, lse, half)
             for piece in range(MODES // WIDTH):
                 load_rows(c, half, piece)
-        if c == 0:
-            share_z(CHUNKS - 1)
     last = CHUNKS - 1
     lse = finish_lse(last)
 
@@ -407,10 +407,8 @@
     for copy in sent:
         copy.wait_send()
     for c in range(CHUNKS):
-        for d, peer in enumerate(x_peers):
-            describe(lse_x.at[c, x], lse_x.at[c, x], LSE_X + c * (NX - 1) + d, peer).wait_send()
-        for d, peer in enumerate(z_peers):
-            describe(lse_z.at[c, z], lse_z.at[c, z], LSE_Z + c * (NZ - 1) + d, peer).wait_send()
+        for copy in share_copies(c):
+            copy.wait_send()
 
 
 def write_out(ks, result, ks_hbm, adjoint_hbm, sem):
@@ -443,8 +441,7 @@
             pltpu.VMEM((STEPS, MODES), BF16),
             pltpu.VMEM((3, MODES, COLS), BF16),
             pltpu.VMEM((GROUPS, STEPS, LANES), F32),
-            pltpu.VMEM((3, STEPS, TILE), F32),
-            pltpu.VMEM((3, STEPS, TILE), F32),
+            pltpu.VMEM((2 * PARTS, 3, PART, TILE), F32),
             pltpu.VMEM((3, STEPS, COLS), F32),
             pltpu.VMEM((STEPS, COLS), F32),
             pltpu.VMEM((BLOCKS, SLABS, 8, LANES), F32),
@@ -458,8 +455,7 @@
             pltpu.VMEM((GROUPS, STEPS, LANES), F32),
             pltpu.VMEM((GROUPS, STEPS, LANES), F32),
             pltpu.VMEM((GROUPS, ROW_BLOCKS, ROWS, LANES), F32),
-            pltpu.VMEM((CHUNKS, NX, CHUNK_BLOCKS, LANES), F32),
-            pltpu.VMEM((CHUNKS, NZ, CHUNK_BLOCKS, LANES), F32),
+            pltpu.VMEM((CHUNKS, NX * NZ, CHUNK_BLOCKS, LANES), F32),
             pltpu.VMEM((NX, 2, MODES), F32),
             pltpu.VMEM((NZ, 2, MODES), F32),
             pltpu.VMEM((2 * NY, 1, MODES), F32),

time: 48.3 us -> 44.8 us (0.928)
  Pallas kernels: 47.5 us -> 44.1 us
    pallas_call x1, Pallas kernels: 46.5 us -> 43.1 us  [body(): pl.pallas_call(kernel, out_shape=(pltpu.VMEM((BLOCKS, LANES), F32), pltpu...]
where the time goes in v4:
time: 44.8 us; the launch traced here: 44.7 us
  Pallas kernels  44.1 us (98%)
  between operations  0.64 us (1%)
    pallas_call x1, Pallas kernels, body(): pl.pallas_call(kernel, out_shape=(pltpu.VMEM((BLOCKS, LANES), F32), pltpu...  43.1 us
    pallas_call x1, Pallas kernels, body(): pl.pallas_call(write_out, out_shape=(jax.ShapeDtypeStruct((BLOCKS, LANES)...  0.99 us

profile of v4, /device:TPU:1, one launch (start us, length us, event | category | flops | bytes accessed | tf_op | source)
XLA Modules:
  0.0 44.7 jit_solution(832334579332842250)
XLA Ops:
  0.6 43.1 %gust_adjoint.1 = (f32[16,128]{1,0:T(8,128)S(1)}, f32[512,512]{1,0:T(8,128)S(1)}) custom-call(bf16[512,512]{1,0:T(8,128)(2,1)} %modal_hbm.1, bf16[3,512,2048]{2,1,0:T(8,128)(2,1)} %modes_hbm.1, f32[512,512]{1,0:T(8,128)} %decay_hbm.1, s32[16]{0:T(128)} %layup_hbm.1, f32[2,16]{1,0:T(2,128)} %bitcast.4, f32[3,16]{1,0:T(4,128)} %bitcast.3, f32[16]{0:T(128)} %base_hbm.1), custom_call_target="tpu_custom_call" | custom-call | tf_op jit(solution)/shard_map/gust_adjoint/pallas_call | solution.py:428
  43.7 1.0 %write_out.1 = (f32[16,128]{1,0:T(8,128)}, f32[512,512]{1,0:T(8,128)}) custom-call(f32[16,128]{1,0:T(8,128)S(1)} %get-tuple-element.6.ks, f32[512,512]{1,0:T(8,128)S(1)} %get-tuple-element.7.result), custom_call_target="tpu_custom_call" | custom-call | tf_op jit(solution)/shard_map/write_out/pallas_call | solution.py:477

commit v5 on v4

--- a/solution.py
+++ b/solution.py
@@ -21,7 +21,7 @@
 PARTS = 1
 PART = STEPS // PARTS
 TILES = COLS // TILE
-CHUNKS = 2
+CHUNKS = 4
 CHUNK_COLS = COLS // CHUNKS
 CHUNK_BLOCKS = BLOCKS // CHUNKS
 SLAB = 64
@@ -255,10 +255,7 @@
 
         sum_tile(first + 1)
 
-        @pl.when(p % 2 == 1)
-        def _():
-            share(p // 2)
-
+        share(p)
         return carry
 
     lax.fori_loop(0, TILES // 2, stress_pair, 0)

time: 44.8 us -> 45.6 us (1.018)
  Pallas kernels: 44.1 us -> 44.9 us
    pallas_call x1, Pallas kernels: 43.1 us -> 43.9 us  [body(): pl.pallas_call(kernel, out_shape=(pltpu.VMEM((BLOCKS, LANES), F32), pltpu...]
where the time goes in v5:
time: 45.6 us; the launch traced here: 45.5 us
  Pallas kernels  44.9 us (98%)
  between operations  0.64 us (1%)
    pallas_call x1, Pallas kernels, body(): pl.pallas_call(kernel, out_shape=(pltpu.VMEM((BLOCKS, LANES), F32), pltpu...  43.9 us
    pallas_call x1, Pallas kernels, body(): pl.pallas_call(write_out, out_shape=(jax.ShapeDtypeStruct((BLOCKS, LANES)...  0.99 us

profile of v5, /device:TPU:1, one launch (start us, length us, event | category | flops | bytes accessed | tf_op | source)
XLA Modules:
  0.0 45.5 jit_solution(4028765450744143387)
XLA Ops:
  0.6 43.9 %gust_adjoint.1 = (f32[16,128]{1,0:T(8,128)S(1)}, f32[512,512]{1,0:T(8,128)S(1)}) custom-call(bf16[512,512]{1,0:T(8,128)(2,1)} %modal_hbm.1, bf16[3,512,2048]{2,1,0:T(8,128)(2,1)} %modes_hbm.1, f32[512,512]{1,0:T(8,128)} %decay_hbm.1, s32[16]{0:T(128)} %layup_hbm.1, f32[2,16]{1,0:T(2,128)} %bitcast.4, f32[3,16]{1,0:T(4,128)} %bitcast.3, f32[16]{0:T(128)} %base_hbm.1), custom_call_target="tpu_custom_call" | custom-call | tf_op jit(solution)/shard_map/gust_adjoint/pallas_call | solution.py:425
  44.5 1.0 %write_out.1 = (f32[16,128]{1,0:T(8,128)}, f32[512,512]{1,0:T(8,128)}) custom-call(f32[16,128]{1,0:T(8,128)S(1)} %get-tuple-element.6.ks, f32[512,512]{1,0:T(8,128)S(1)} %get-tuple-element.7.result), custom_call_target="tpu_custom_call" | custom-call | tf_op jit(solution)/shard_map/write_out/pallas_call | solution.py:474

commit v6 on v4

--- a/solution.py
+++ b/solution.py
@@ -38,14 +38,14 @@
 NT = (((1,), (1,)), ((), ()))
 
 LSE = 0
-PAIR = LSE + CHUNKS * (NX * NZ - 1)
+PAIR = LSE + CHUNKS
 RING = PAIR + GROUPS
-CARRY_X = RING + (NY - 1) * GROUPS
-CARRY_Z = CARRY_X + NX - 1
-INCOMING = CARRY_Z + NZ - 1
-SPREAD = INCOMING + 2 * NY - 1
-ACROSS = SPREAD + (NY - 1) * GROUPS
-SENDS = ACROSS + NY * GROUPS
+CARRY_X = RING + GROUPS
+CARRY_Z = CARRY_X + 1
+INCOMING = CARRY_Z + 1
+SPREAD = INCOMING + 1
+ACROSS = SPREAD + GROUPS
+RECEIVES = ACROSS + GROUPS
 
 MODAL_IN = TILES
 DECAY_IN = TILES + 1
@@ -78,21 +78,20 @@
     ring = [(tm, 2 * q + core) for q in (y_far, y_up, y_down)]
     ring_y = (y_far, y_down, y_up)
 
-    sent = []
-
-    def describe(src, dst, slot, peer):
+    def describe(src, dst, send_slot, slot, peer):
         return pltpu.make_async_remote_copy(
-            src_ref=src, dst_ref=dst, send_sem=send_sem.at[slot], recv_sem=recv_sem.at[slot],
+            src_ref=src, dst_ref=dst, send_sem=send_sem.at[send_slot], recv_sem=recv_sem.at[slot],
             device_id=peer, device_id_type=MESH,
         )
 
-    def send(src, dst, slot, peer):
-        copy = describe(src, dst, slot, peer)
-        copy.start()
-        sent.append(copy)
-
-    def arrived(dst, slot):
-        describe(dst, dst, slot, pair).wait_recv()
+    def send(src, dst, send_slot, slot, peer):
+        describe(src, dst, send_slot, slot, peer).start()
+
+    def arrived(extent, slot):
+        describe(extent, extent, 0, slot, pair).wait_recv()
+
+    def gone(extent, send_slot):
+        describe(extent, extent, send_slot, 0, pair).wait_send()
 
     table_copies = [
         pltpu.make_async_copy(src, dst, in_sem.at[TABLE_IN + i])
@@ -184,24 +183,18 @@
         top = jnp.max(values, axis=0)
         return top + log_two(jnp.sum(jnp.exp2(values - top[None]), axis=0))
 
-    def share_copies(c):
-        for d, (dz, dx) in enumerate(offsets_zx):
-            peer = (((z + dz) % NZ) * NX + (x + dx) % NX, elem)
-            yield describe(shares.at[c, tm], shares.at[c, tm], LSE + c * (NX * NZ - 1) + d, peer)
-
     def share(c):
         blocks = pl.ds(c * CHUNK_BLOCKS, CHUNK_BLOCKS)
         tops = block_max[blocks]
         top = jnp.max(tops, axis=1)
         total = jnp.sum(block_sum[blocks] * jnp.exp2(tops - top[:, None, :]), axis=1)
         shares[c, tm] = top + log_two(total)
-        for copy in share_copies(c):
-            copy.start()
+        for dz, dx in offsets_zx:
+            peer = (((z + dz) % NZ) * NX + (x + dx) % NX, elem)
+            send(shares.at[c, tm], shares.at[c, tm], LSE + c, LSE + c, peer)
 
     def finish_lse(c):
-        for d, (dz, dx) in enumerate(offsets_zx):
-            source = ((z + NZ - dz) % NZ) * NX + (x + NX - dx) % NX
-            arrived(shares.at[c, source], LSE + c * (NX * NZ - 1) + d)
+        arrived(shares.at[c, pl.ds(0, NX * NZ - 1)], LSE + c)
         lse = log_sum(shares[c])
         for b in range(CHUNK_BLOCKS):
             block = c * CHUNK_BLOCKS + b
@@ -303,7 +296,7 @@
     for piece in range(MODES // WIDTH):
         load_rows(last, 1 - core, piece)
         for g in range(piece * PER_DOT, (piece + 1) * PER_DOT):
-            send(loads.at[g, pair_rows, :], pair_in.at[g], PAIR + g, pair)
+            send(loads.at[g, pair_rows, :], pair_in.at[g], PAIR, PAIR + g, pair)
     weigh(last, lse, core)
     for piece in range(MODES // WIDTH):
         load_rows(last, core, piece)
@@ -317,7 +310,7 @@
         arrived(pair_in.at[g], PAIR + g)
         for i, q in enumerate((y_far, y_up, y_down)):
             partial[g, i] = pair_sum(g, q)
-            send(partial.at[g, i], near_in.at[g, i], RING + (NY - 1) * g + i, ring[i])
+            send(partial.at[g, i], near_in.at[g, i], RING, RING + g, ring[i])
 
     for g in range(GROUPS):
         ahead = jnp.ones((1, LANES), F32)
@@ -329,11 +322,10 @@
             ahead = ahead * tail_prod[g, r * ROWS : r * ROWS + 1, :]
         carry_x[x, 0:1, pl.ds(g * LANES, LANES)] = ahead
         carry_x[x, 1:2, pl.ds(g * LANES, LANES)] = state
-    for d, peer in enumerate(x_peers):
-        send(carry_x.at[x], carry_x.at[x], CARRY_X + d, peer)
-
-    for d in range(NX - 1):
-        arrived(carry_x.at[(x + NX - 1 - d) % NX], CARRY_X + d)
+    for peer in x_peers:
+        send(carry_x.at[x], carry_x.at[x], CARRY_X, CARRY_X, peer)
+
+    arrived(carry_x.at[pl.ds(0, NX - 1)], CARRY_X)
     slab_scale = jnp.ones((1, MODES), F32)
     slab_state = jnp.zeros((1, MODES), F32)
     later_scale, later_state = slab_scale, slab_state
@@ -345,18 +337,17 @@
         later_scale = jnp.where(q > x, scale * later_scale, later_scale)
     carry_z[z, 0:1, :] = slab_scale
     carry_z[z, 1:2, :] = slab_state
-    for d, peer in enumerate(z_peers):
-        send(carry_z.at[z], carry_z.at[z], CARRY_Z + d, peer)
+    for peer in z_peers:
+        send(carry_z.at[z], carry_z.at[z], CARRY_Z, CARRY_Z, peer)
 
     mine = core * NY + y
 
-    def spread(g, block, slot, peer):
-        send(offsets.at[g, block], offsets.at[g, block], slot, peer)
+    def spread(g, block, send_slot, slot, peer):
+        send(offsets.at[g, block], offsets.at[g, block], send_slot, slot, peer)
 
     mine_rows = pl.ds(pl.multiple_of(mine * ROWS, ROWS), ROWS)
     for g in range(GROUPS):
-        for i in range(NY - 1):
-            arrived(near_in.at[g, i], RING + (NY - 1) * g + i)
+        arrived(near_in.at[g], RING + g)
         state = (pair_sum(g, y) + near_in[g, 1]) + (near_in[g, 2] + near_in[g, 0])
         state = state.reshape(tiles, 8, LANES)
         factor = decay[g, mine_rows, :].reshape(tiles, 8, LANES)
@@ -370,33 +361,29 @@
             offsets[g, mine, pl.ds(m * 8, 8), :] = value
             running = value[0:1]
         for i in range(NY - 1):
-            spread(g, mine, SPREAD + (NY - 1) * g + i, ring[i])
-        spread(g, mine, ACROSS + NY * g, pair)
-
-    for d in range(NZ - 1):
-        arrived(carry_z.at[(z + NZ - 1 - d) % NZ], CARRY_Z + d)
+            spread(g, mine, SPREAD, SPREAD + g, ring[i])
+        spread(g, mine, ACROSS, ACROSS + g, pair)
+
+    arrived(carry_z.at[pl.ds(0, NZ - 1)], CARRY_Z)
     far_state = jnp.zeros((1, MODES), F32)
     for q in range(NZ - 1, -1, -1):
         far_state = jnp.where(q > z, carry_z[q, 1:2, :] + carry_z[q, 0:1, :] * far_state, far_state)
     incoming[elem] = later_state + later_scale * far_state
-    for d, peer in enumerate(elem_peers):
-        send(incoming.at[elem], incoming.at[elem], INCOMING + d, peer)
-
-    for g in range(GROUPS):
-        for i, q in enumerate(ring_y):
-            arrived(offsets.at[g, core * NY + q], SPREAD + (NY - 1) * g + i)
-            spread(g, core * NY + q, ACROSS + NY * g + 1 + i, pair)
-
-    for d in range(2 * NY - 1):
-        arrived(incoming.at[(elem + 2 * NY - 1 - d) % (2 * NY)], INCOMING + d)
+    for peer in elem_peers:
+        send(incoming.at[elem], incoming.at[elem], INCOMING, INCOMING, peer)
+
+    for g in range(GROUPS):
+        arrived(offsets.at[g, pl.ds(0, NY - 1)], SPREAD + g)
+        for q in ring_y:
+            spread(g, core * NY + q, ACROSS, ACROSS + g, pair)
+
+    arrived(incoming.at[pl.ds(0, 2 * NY - 1)], INCOMING)
     behind = incoming[0]
     for e in range(1, 2 * NY):
         behind = behind + incoming[e]
 
-    other = (1 - core) * NY
-    for g in range(GROUPS):
-        for i, q in enumerate((y,) + ring_y):
-            arrived(offsets.at[g, other + q], ACROSS + NY * g + i)
+    for g in range(GROUPS):
+        arrived(offsets.at[g, pl.ds(0, NY)], ACROSS + g)
         there = pl.ds(g * LANES, LANES)
         state = behind[:, g * LANES : (g + 1) * LANES]
         for r in range(ROW_BLOCKS - 1, -1, -1):
@@ -404,11 +391,15 @@
             result[rows, there] = offsets[g, r] + tail_prod[g, rows, :] * state
             state = offsets[g, r, 0:1, :] + tail_prod[g, r * ROWS : r * ROWS + 1, :] * state
 
-    for copy in sent:
-        copy.wait_send()
     for c in range(CHUNKS):
-        for copy in share_copies(c):
-            copy.wait_send()
+        gone(shares.at[c, pl.ds(0, NX * NZ - 1)], LSE + c)
+    gone(pair_in, PAIR)
+    gone(partial, RING)
+    gone(carry_x.at[pl.ds(0, NX - 1)], CARRY_X)
+    gone(carry_z.at[pl.ds(0, NZ - 1)], CARRY_Z)
+    gone(incoming.at[pl.ds(0, 2 * NY - 1)], INCOMING)
+    gone(offsets.at[:, pl.ds(0, NY - 1)], SPREAD)
+    gone(offsets.at[:, pl.ds(0, NY)], ACROSS)
 
 
 def write_out(ks, result, ks_hbm, adjoint_hbm, sem):
@@ -460,8 +451,8 @@
             pltpu.VMEM((NZ, 2, MODES), F32),
             pltpu.VMEM((2 * NY, 1, MODES), F32),
             pltpu.SemaphoreType.DMA((INPUTS,)),
-            pltpu.SemaphoreType.DMA((SENDS,)),
-            pltpu.SemaphoreType.DMA((SENDS,)),
+            pltpu.SemaphoreType.DMA((RECEIVES,)),
+            pltpu.SemaphoreType.DMA((RECEIVES,)),
         ],
         compiler_params=pltpu.CompilerParams(
             collective_id=0, has_side_effects=True, vmem_limit_bytes=48 * 1024 * 1024

time: 44.8 us -> 42.8 us (0.955)
  Pallas kernels: 44.1 us -> 42.1 us
    pallas_call x1, Pallas kernels: 43.1 us -> 41.1 us  [body(): pl.pallas_call(kernel, out_shape=(pltpu.VMEM((BLOCKS, LANES), F32), pltpu...]
where the time goes in v6:
time: 42.8 us; the launch traced here: 42.7 us
  Pallas kernels  42.1 us (98%)
  between operations  0.64 us (1%)
    pallas_call x1, Pallas kernels, body(): pl.pallas_call(kernel, out_shape=(pltpu.VMEM((BLOCKS, LANES), F32), pltpu...  41.1 us
    pallas_call x1, Pallas kernels, body(): pl.pallas_call(write_out, out_shape=(jax.ShapeDtypeStruct((BLOCKS, LANES)...  0.99 us

profile of v6, /device:TPU:1, one launch (start us, length us, event | category | flops | bytes accessed | tf_op | source)
XLA Modules:
  0.0 42.7 jit_solution(6299808333725897481)
XLA Ops:
  0.6 41.1 %gust_adjoint.1 = (f32[16,128]{1,0:T(8,128)S(1)}, f32[512,512]{1,0:T(8,128)S(1)}) custom-call(bf16[512,512]{1,0:T(8,128)(2,1)} %modal_hbm.1, bf16[3,512,2048]{2,1,0:T(8,128)(2,1)} %modes_hbm.1, f32[512,512]{1,0:T(8,128)} %decay_hbm.1, s32[16]{0:T(128)} %layup_hbm.1, f32[2,16]{1,0:T(2,128)} %bitcast.4, f32[3,16]{1,0:T(4,128)} %bitcast.3, f32[16]{0:T(128)} %base_hbm.1), custom_call_target="tpu_custom_call" | custom-call | tf_op jit(solution)/shard_map/gust_adjoint/pallas_call | solution.py:419
  41.7 1.0 %write_out.1 = (f32[16,128]{1,0:T(8,128)}, f32[512,512]{1,0:T(8,128)}) custom-call(f32[16,128]{1,0:T(8,128)S(1)} %get-tuple-element.6.ks, f32[512,512]{1,0:T(8,128)S(1)} %get-tuple-element.7.result), custom_call_target="tpu_custom_call" | custom-call | tf_op jit(solution)/shard_map/write_out/pallas_call | solution.py:468

commit v7 on v6

--- a/solution.py
+++ b/solution.py
@@ -21,7 +21,7 @@
 PARTS = 1
 PART = STEPS // PARTS
 TILES = COLS // TILE
-CHUNKS = 2
+CHUNKS = 4
 CHUNK_COLS = COLS // CHUNKS
 CHUNK_BLOCKS = BLOCKS // CHUNKS
 SLAB = 64
@@ -248,10 +248,7 @@
 
         sum_tile(first + 1)
 
-        @pl.when(p % 2 == 1)
-        def _():
-            share(p // 2)
-
+        share(p)
         return carry
 
     lax.fori_loop(0, TILES // 2, stress_pair, 0)

time: 42.8 us -> 42.4 us (level)
  no operation moved by 1% of the time
where the time goes in v7:
time: 42.4 us; the launch traced here: 42.3 us
  Pallas kernels  41.7 us (98%)
  between operations  0.64 us (2%)
    pallas_call x1, Pallas kernels, body(): pl.pallas_call(kernel, out_shape=(pltpu.VMEM((BLOCKS, LANES), F32), pltpu...  40.7 us
    pallas_call x1, Pallas kernels, body(): pl.pallas_call(write_out, out_shape=(jax.ShapeDtypeStruct((BLOCKS, LANES)...  0.99 us

profile of v7, /device:TPU:1, one launch (start us, length us, event | category | flops | bytes accessed | tf_op | source)
XLA Modules:
  0.0 42.3 jit_solution(13709198144431910722)
XLA Ops:
  0.6 40.7 %gust_adjoint.1 = (f32[16,128]{1,0:T(8,128)S(1)}, f32[512,512]{1,0:T(8,128)S(1)}) custom-call(bf16[512,512]{1,0:T(8,128)(2,1)} %modal_hbm.1, bf16[3,512,2048]{2,1,0:T(8,128)(2,1)} %modes_hbm.1, f32[512,512]{1,0:T(8,128)} %decay_hbm.1, s32[16]{0:T(128)} %layup_hbm.1, f32[2,16]{1,0:T(2,128)} %bitcast.4, f32[3,16]{1,0:T(4,128)} %bitcast.3, f32[16]{0:T(128)} %base_hbm.1), custom_call_target="tpu_custom_call" | custom-call | tf_op jit(solution)/shard_map/gust_adjoint/pallas_call | solution.py:416
  41.3 1.0 %write_out.1 = (f32[16,128]{1,0:T(8,128)}, f32[512,512]{1,0:T(8,128)}) custom-call(f32[16,128]{1,0:T(8,128)S(1)} %get-tuple-element.6.ks, f32[512,512]{1,0:T(8,128)S(1)} %get-tuple-element.7.result), custom_call_target="tpu_custom_call" | custom-call | tf_op jit(solution)/shard_map/write_out/pallas_call | solution.py:465

commit v8 on v7

--- a/solution.py
+++ b/solution.py
@@ -401,9 +401,11 @@
 
 def write_out(ks, result, ks_hbm, adjoint_hbm, sem):
     copies = [
-        pltpu.make_async_copy(result, adjoint_hbm, sem.at[0]),
-        pltpu.make_async_copy(ks, ks_hbm, sem.at[1]),
-    ]
+        pltpu.make_async_copy(
+            result.at[pl.ds(r * ROWS, ROWS), :], adjoint_hbm.at[pl.ds(r * ROWS, ROWS), :], sem.at[r]
+        )
+        for r in range(ROW_BLOCKS)
+    ] + [pltpu.make_async_copy(ks, ks_hbm, sem.at[ROW_BLOCKS])]
     for copy in copies:
         copy.start()
     for copy in copies:
@@ -470,7 +472,7 @@
         ),
         in_specs=[vmem] * 2,
         out_specs=(hbm, hbm),
-        scratch_shapes=[pltpu.SemaphoreType.DMA((2,))],
+        scratch_shapes=[pltpu.SemaphoreType.DMA((ROW_BLOCKS + 1,))],
         name="write_out",
     )(
         pltpu.with_memory_space_constraint(ks, pltpu.VMEM),

time: 42.4 us -> 42.5 us (level)
  no operation moved by 1% of the time
where the time goes in v8:
time: 42.5 us; the launch traced here: 42.4 us
  Pallas kernels  41.7 us (98%)
  between operations  0.64 us (2%)
    pallas_call x1, Pallas kernels, body(): pl.pallas_call(kernel, out_shape=(pltpu.VMEM((BLOCKS, LANES), F32), pltpu...  40.7 us
    pallas_call x1, Pallas kernels, body(): pl.pallas_call(write_out, out_shape=(jax.ShapeDtypeStruct((BLOCKS, LANES)...  1.04 us

profile of v8, /device:TPU:1, one launch (start us, length us, event | category | flops | bytes accessed | tf_op | source)
XLA Modules:
  0.0 42.4 jit_solution(3327661399805443981)
XLA Ops:
  0.6 40.7 %gust_adjoint.1 = (f32[16,128]{1,0:T(8,128)S(1)}, f32[512,512]{1,0:T(8,128)S(1)}) custom-call(bf16[512,512]{1,0:T(8,128)(2,1)} %modal_hbm.1, bf16[3,512,2048]{2,1,0:T(8,128)(2,1)} %modes_hbm.1, f32[512,512]{1,0:T(8,128)} %decay_hbm.1, s32[16]{0:T(128)} %layup_hbm.1, f32[2,16]{1,0:T(2,128)} %bitcast.4, f32[3,16]{1,0:T(4,128)} %bitcast.3, f32[16]{0:T(128)} %base_hbm.1), custom_call_target="tpu_custom_call" | custom-call | tf_op jit(solution)/shard_map/gust_adjoint/pallas_call | solution.py:418
  41.3 1.0 %write_out.1 = (f32[16,128]{1,0:T(8,128)}, f32[512,512]{1,0:T(8,128)}) custom-call(f32[16,128]{1,0:T(8,128)S(1)} %get-tuple-element.6.ks, f32[512,512]{1,0:T(8,128)S(1)} %get-tuple-element.7.result), custom_call_target="tpu_custom_call" | custom-call | tf_op jit(solution)/shard_map/write_out/pallas_call | solution.py:467

commit v9 on v7

--- a/solution.py
+++ b/solution.py
@@ -207,17 +207,16 @@
             rows = pl.ds(pl.multiple_of(r * SLAB, SLAB), SLAB)
             for b in range(CHUNK_BLOCKS):
                 there = pl.ds((c * CHUNK_BLOCKS + b) * LANES, LANES)
-                here = pl.ds(b * LANES, LANES)
                 weight = jnp.exp2(index[rows, there] - lse[b : b + 1])
                 for k in range(3):
-                    sens[k, rows, here] = (weight * graded[k, rows, there]).astype(BF16)
+                    sens[k, b, rows, :] = (weight * graded[k, rows, there]).astype(BF16)
 
     def load_rows(c, half, piece):
         rows = pl.ds(pl.multiple_of(half * (STEPS // 2), STEPS // 2), STEPS // 2)
         total = None
         for k in range(3):
             part = lax.dot_general(
-                sens[k, rows, :],
+                jnp.concatenate([sens[k, b, rows, :] for b in range(CHUNK_BLOCKS)], axis=1),
                 modes[k, pl.ds(piece * WIDTH, WIDTH), pl.ds(c * CHUNK_COLS, CHUNK_COLS)],
                 NT, preferred_element_type=F32,
             )
@@ -435,7 +434,7 @@
             pltpu.VMEM((BLOCKS, SLABS, 8, LANES), F32),
             pltpu.VMEM((BLOCKS, 8, LANES), F32),
             pltpu.VMEM((BLOCKS, 8, LANES), F32),
-            pltpu.VMEM((3, STEPS, CHUNK_COLS), BF16),
+            pltpu.VMEM((3, CHUNK_BLOCKS, STEPS, LANES), BF16),
             pltpu.VMEM((GROUPS, STEPS, LANES), F32),
             pltpu.VMEM((GROUPS, STEPS // 2, LANES), F32),
             pltpu.VMEM((GROUPS, NY - 1, ROWS, LANES), F32),

time: 42.4 us -> 42.4 us (level)
  no operation moved by 1% of the time
where the time goes in v9:
time: 42.4 us; the launch traced here: 42.3 us
  Pallas kernels  41.7 us (98%)
  between operations  0.64 us (2%)
    pallas_call x1, Pallas kernels, body(): pl.pallas_call(kernel, out_shape=(pltpu.VMEM((BLOCKS, LANES), F32), pltpu...  40.7 us
    pallas_call x1, Pallas kernels, body(): pl.pallas_call(write_out, out_shape=(jax.ShapeDtypeStruct((BLOCKS, LANES)...  0.99 us

profile of v9, /device:TPU:1, one launch (start us, length us, event | category | flops | bytes accessed | tf_op | source)
XLA Modules:
  0.0 42.3 jit_solution(790391612153073721)
XLA Ops:
  0.6 40.7 %gust_adjoint.1 = (f32[16,128]{1,0:T(8,128)S(1)}, f32[512,512]{1,0:T(8,128)S(1)}) custom-call(bf16[512,512]{1,0:T(8,128)(2,1)} %modal_hbm.1, bf16[3,512,2048]{2,1,0:T(8,128)(2,1)} %modes_hbm.1, f32[512,512]{1,0:T(8,128)} %decay_hbm.1, s32[16]{0:T(128)} %layup_hbm.1, f32[2,16]{1,0:T(2,128)} %bitcast.4, f32[3,16]{1,0:T(4,128)} %bitcast.3, f32[16]{0:T(128)} %base_hbm.1), custom_call_target="tpu_custom_call" | custom-call | tf_op jit(solution)/shard_map/gust_adjoint/pallas_call | solution.py:415
  41.3 1.0 %write_out.1 = (f32[16,128]{1,0:T(8,128)}, f32[512,512]{1,0:T(8,128)}) custom-call(f32[16,128]{1,0:T(8,128)S(1)} %get-tuple-element.6.ks, f32[512,512]{1,0:T(8,128)S(1)} %get-tuple-element.7.result), custom_call_target="tpu_custom_call" | custom-call | tf_op jit(solution)/shard_map/write_out/pallas_call | solution.py:464
